TPU v7x, 128 devices: a whole 4x4x4 slice. The times are simulated.
128 devices in a mesh: row: 16 (over z_lo, y, core), col: 8 (over z_hi, x).
Axes of the slice: x: 4, y: 4, z: 4 (z_hi: 2, z_lo: 2; z = z_hi * 2 + z_lo), core: 2. Of those that a mesh axis runs over, the one named last changes fastest.
Arguments:
- hidden: bfloat16 [6144, 5120], P('row', 'col'), may hold values from -6 to 6
- modulation: float32 [2, 5120], replicated, may hold values from -3 to 3
- w_query: bfloat16 [5120, 5120], P('row', 'col'), may hold values from -2 to 2
- w_key: bfloat16 [5120, 5120], P('row', 'col'), may hold values from -2 to 2
- w_value: bfloat16 [5120, 5120], P('row', 'col'), may hold values from -0.078125 to 0.078125
- q_gain: float32 [5120], P('col'), may hold values from 0.4 to 4.3
- k_gain: float32 [5120], P('col'), may hold values from 0.4 to 4.3
- positions: int32 [3, 6144], P(None, 'row'), may hold values from 0 to 63
- segment_ids: int32 [6144], replicated, may hold values from 0 to 11, never falling along the last dimension, each value on 1 to 3072 neighbouring positions
- page_table: int32 [48], replicated, may hold values from 0 to 47, each once
Outputs:
- attended: bfloat16 [6144, 5120], P('row', 'col')
- page_store: bfloat16 [2, 48, 128, 5120], P(None, 'row', None, 'col')
Inputs may be any that keep to these rules, and one draw needn't show every extreme that they name: `segment_ids`: segment numbers never fall along the tokens; each segment holds at most 3072 tokens, and one holds exactly 3072. `page_table`: every slot is named by exactly one block.
All inputs are finite; a program needn't handle non-finite values.
Results may differ from a plain program's by a relative error of at most 0.015.
Values may be sent and summed in bfloat16 or wider, within the bound.
A program may use at most 128 MiB of HBM per device.

v0:
```python
import jax
import jax.numpy as jnp
from jax import lax
from jax.sharding import PartitionSpec as P

HEAD_DIM = 128
PAGE = 128


epsilon = 1e-06


def rotary_table(positions, pair_count):
    frame_pairs = pair_count - 2 * (pair_count // 3)
    side_pairs = pair_count // 3
    column = jnp.arange(pair_count)
    frame_rate = 10000.0 ** (-column.astype(jnp.float32) / frame_pairs)
    height_rate = 10000.0 ** (-(column - frame_pairs).astype(jnp.float32) / side_pairs)
    width_rate = 10000.0 ** (-(column - frame_pairs - side_pairs).astype(jnp.float32) / side_pairs)
    coords = positions.astype(jnp.float32)
    angles = jnp.where(
        column < frame_pairs,
        coords[0][:, None] * frame_rate,
        jnp.where(
            column < frame_pairs + side_pairs,
            coords[1][:, None] * height_rate,
            coords[2][:, None] * width_rate,
        ),
    )
    return (jnp.cos(angles), jnp.sin(angles))


def rotate(values, cosine, sine_table, head_dim):
    row_count = values.shape[0]
    head_count = values.shape[1] // head_dim
    paired = values.reshape(row_count, head_count, head_dim // 2, 2)
    former = paired[..., 0]
    latter = paired[..., 1]
    cosine = cosine[:, None, :]
    sine_table = sine_table[:, None, :]
    turned = jnp.stack(
        [former * cosine - latter * sine_table, former * sine_table + latter * cosine], axis=-1
    )
    return turned.reshape(row_count, head_count * head_dim)


def modulate(activations, modulation):
    average = jnp.mean(activations, axis=1, keepdims=True)
    centred = activations - average
    variance = jnp.mean(centred * centred, axis=1, keepdims=True)
    normed = centred * lax.rsqrt(variance + epsilon)
    return (normed * (1.0 + modulation[1]) + modulation[0]).astype(jnp.bfloat16)


def blockwise(columns, weight_blocks):
    partial_value = jnp.einsum(
        "tnf,nfo->nto", columns, weight_blocks, preferred_element_type=jnp.float32
    )
    partial_value = lax.optimization_barrier(partial_value.astype(jnp.bfloat16))
    return jnp.sum(partial_value.astype(jnp.float32), axis=0)


def body(
    hidden, modulation, w_query, w_key, w_value, q_gain, k_gain, positions, segment_ids, page_table
):
    full_rows = lax.all_gather(hidden, "col", axis=1, tiled=True)
    modulated = modulate(full_rows.astype(jnp.float32), modulation)
    tok_rows = hidden.shape[0]
    shard_rows = w_query.shape[0]
    local_cols = w_query.shape[1]
    full_width = full_rows.shape[1]
    head_dim = HEAD_DIM
    gathered = (
        lax.all_gather(w_query, "row", axis=0, tiled=True),
        lax.all_gather(w_key, "row", axis=0, tiled=True),
        lax.all_gather(w_value, "row", axis=0, tiled=True),
    )
    blocks = full_width // shard_rows
    columns = modulated.reshape(tok_rows, blocks, shard_rows)
    query_raw = blockwise(columns, gathered[0].reshape(blocks, shard_rows, local_cols))
    key_raw = blockwise(columns, gathered[1].reshape(blocks, shard_rows, local_cols))
    value_raw = blockwise(columns, gathered[2].reshape(blocks, shard_rows, local_cols))
    squares = lax.psum(
        (jnp.sum(query_raw * query_raw, axis=1), jnp.sum(key_raw * key_raw, axis=1)), "col"
    )
    query_normed = query_raw * lax.rsqrt(squares[0][:, None] / full_width + epsilon) * q_gain
    key_normed = key_raw * lax.rsqrt(squares[1][:, None] / full_width + epsilon) * k_gain
    cosine, sine_table = rotary_table(positions, head_dim // 2)
    query = rotate(query_normed, cosine, sine_table, head_dim).astype(jnp.bfloat16)
    key = rotate(key_normed, cosine, sine_table, head_dim).astype(jnp.bfloat16)
    value = value_raw.astype(jnp.bfloat16)
    keys_all, values_all = (
        lax.all_gather(key, "row", axis=0, tiled=True),
        lax.all_gather(value, "row", axis=0, tiled=True),
    )
    row_index = lax.axis_index("row")
    query_segs = lax.dynamic_slice_in_dim(segment_ids, row_index * tok_rows, tok_rows, 0)
    local_heads = local_cols // head_dim
    query_tile = query.reshape(tok_rows, local_heads, head_dim)
    key_block = min(512, keys_all.shape[0])
    block_total = keys_all.shape[0] // key_block

    def attend_block(number, carry):
        running, totals, weighted = carry
        offset = number * key_block
        key_tile = lax.dynamic_slice_in_dim(keys_all, offset, key_block, 0).reshape(
            key_block, local_heads, head_dim
        )
        value_tile = lax.dynamic_slice_in_dim(values_all, offset, key_block, 0).reshape(
            key_block, local_heads, head_dim
        )
        block_segs = lax.dynamic_slice_in_dim(segment_ids, offset, key_block, 0)
        scores = jnp.einsum(
            "qhd,khd->qhk", query_tile, key_tile, preferred_element_type=jnp.float32
        ) * head_dim ** (-0.5)
        allowed = (query_segs[:, None] == block_segs[None, :])[:, None, :]
        newest = jnp.maximum(running, jnp.max(jnp.where(allowed, scores, -1e30), axis=2))
        weights = jnp.where(allowed, jnp.exp(scores - newest[..., None]), 0.0)
        factor = jnp.exp(running - newest)
        totals = totals * factor + jnp.sum(weights, axis=2)
        weighted = weighted * factor[..., None] + jnp.einsum(
            "qhk,khd->qhd",
            weights.astype(jnp.bfloat16),
            value_tile,
            preferred_element_type=jnp.float32,
        )
        return (newest, totals, weighted)

    starting = (
        jnp.full((tok_rows, local_heads), -1e30, jnp.float32),
        jnp.zeros((tok_rows, local_heads), jnp.float32),
        jnp.zeros((tok_rows, local_heads, head_dim), jnp.float32),
    )
    first_block = 0
    running, totals, weighted = lax.fori_loop(first_block, block_total, attend_block, starting)
    attended = (weighted / totals[..., None]).reshape(tok_rows, local_cols).astype(jnp.bfloat16)
    own_pages = tok_rows // PAGE
    page_count = page_table.shape[0]
    inverse = (
        jnp.zeros((page_count,), jnp.int32)
        .at[page_table]
        .set(jnp.arange(page_count, dtype=jnp.int32))
    )
    owned = lax.dynamic_slice_in_dim(inverse, row_index * own_pages, own_pages, 0)
    key_pages = keys_all.reshape(page_count, PAGE, local_cols)[owned]
    value_pages = values_all.reshape(page_count, PAGE, local_cols)[owned]
    return (attended, jnp.stack([key_pages, value_pages]))


def solution(mesh):
    in_specs = (
        P("row", "col"),
        P(),
        P("row", "col"),
        P("row", "col"),
        P("row", "col"),
        P("col"),
        P("col"),
        P(None, "row"),
        P(),
        P(),
    )
    out_specs = (P("row", "col"), P(None, "row", None, "col"))
    return jax.shard_map(body, mesh=mesh, in_specs=in_specs, out_specs=out_specs, check_vma=False)
```

profile of v0, /device:TPU:1, one launch (start us, length us, event | category | flops | bytes accessed | tf_op | source)
XLA Modules:
  0.0 501.0 jit_solution(13298222209853916051)
XLA Ops:
  17.1 66.0 %all-gather.7.cloned.1.call-done = bf16[384,5120]{0,1:T(8,128)(2,1)} async-done(((bf16[384,640]{0,1:T(8,128)(2,1)}), bf16[384,5120]{0,1:T(8,128)(2,1)}) %all-gather.7.cloned.1.call-update) | async-done | bytes 3932176 | tf_op jit(solution)/shard_map/all_gather | solution.py:66
  83.1 3.0 convert_reduce_fusion.2
  87.5 4.0 fusion.25
  91.6 35.4 %all-gather.13.cloned.1.call-done = bf16[5120,640]{1,0:T(8,128)(2,1)} async-done(((bf16[320,640]{1,0:T(8,128)(2,1)}), bf16[5120,640]{1,0:T(8,128)(2,1)}) %all-gather.13.cloned.1.call-update) | async-done | bytes 6553616 | tf_op jit(solution)/shard_map/all_gather | solution.py:74
  126.9 11.8 %convolution_convert_fusion.1 = bf16[16,384,640]{2,1,0:T(8,128)(2,1)} fusion(bf16[384,16,320]{0,2,1:T(8,128)(2,1)} %bitcast.71, bf16[16,320,640]{2,1,0:T(8,128)(2,1)} %bitcast.77), kind=kOutput, calls=%fused_computation.38 | convolution fusion | flops 2520514560 | bytes 18350080 | tf_op jit(solution)/shard_map/tnf,nfo->nto/dot_general | solution.py:56
  138.8 34.3 %all-gather.9.cloned.1.call-done = bf16[5120,640]{1,0:T(8,128)(2,1)} async-done(((bf16[320,640]{1,0:T(8,128)(2,1)}), bf16[5120,640]{1,0:T(8,128)(2,1)}) %all-gather.9.cloned.1.call-update) | async-done | bytes 6553616 | tf_op jit(solution)/shard_map/all_gather | solution.py:75
  173.1 8.7 %convolution_convert_fusion.2 = bf16[16,384,640]{2,1,0:T(8,128)(2,1)S(1)} fusion(bf16[384,16,320]{0,2,1:T(8,128)(2,1)} %bitcast.72, bf16[16,320,640]{2,1,0:T(8,128)(2,1)} %bitcast.78), kind=kOutput, calls=%fused_computation.39 | convolution fusion | flops 2520514560 | bytes 18350080 | tf_op jit(solution)/shard_map/tnf,nfo->nto/dot_general | solution.py:56
  183.9 4.9 convert_reduce_fusion
  193.1 20.8 %all-reduce = (f32[384]{0:T(512)S(1)}, f32[384]{0:T(512)S(1)}) all-reduce(f32[384]{0:T(512)S(1)} %multiply_reduce_fusion.1, f32[384]{0:T(512)S(1)} %multiply_reduce_fusion), channel_id=1, replica_groups=mesh['row'=16,'col'=8] {'col'}, use_global_device_ids=true, to_apply=%region_4.0 | all-reduce | flops 768 | bytes 6144 | tf_op jit(solution)/shard_map/psum | solution.py:83
  216.1 3.4 subtract_convert_fusion
  221.7 11.9 %convolution_convert_fusion = bf16[16,384,640]{2,1,0:T(8,128)(2,1)} fusion(bf16[384,16,320]{0,2,1:T(8,128)(2,1)} %bitcast.73, bf16[16,320,640]{2,1,0:T(8,128)(2,1)} %bitcast.76), kind=kOutput, calls=%fused_computation.37 | convolution fusion | flops 2520514560 | bytes 18350080 | tf_op jit(solution)/shard_map/tnf,nfo->nto/dot_general | solution.py:56
  233.6 5.4 %reduce_sum.91 = bf16[384,640]{1,0:T(8,128)(2,1)} reduce(bf16[16,384,640]{2,1,0:T(8,128)(2,1)} %convolution_convert_fusion, bf16[]{:T(256)} %constant.102.clone.1), dimensions={0}, to_apply=%region_5.0 | reduce | flops 3686400 | bytes 8355842 | tf_op jit(solution)/shard_map/reduce_sum | solution.py:60
  242.6 29.1 %all-gather.11.cloned.1.call-done = bf16[6144,640]{0,1:T(8,128)(2,1)} async-done(((bf16[384,640]{0,1:T(8,128)(2,1)}), bf16[6144,640]{0,1:T(8,128)(2,1)}) %all-gather.11.cloned.1.call-update) | async-done | bytes 7864336 | tf_op jit(solution)/shard_map/all_gather | solution.py:93
  271.6 10.4 %copy.38 = bf16[6144,640]{1,0:T(8,128)(2,1)} copy(bf16[6144,640]{0,1:T(8,128)(2,1)} %all-gather.11.cloned.1.call-done) | data formatting | bytes 15728640 | tf_op jit(solution)/shard_map/all_gather | solution.py:93
  282.1 4.2 gather_fusion
  286.3 37.5 %all-gather.17.cloned.1.call-done = bf16[6144,640]{1,0:T(8,128)(2,1)} async-done(((bf16[384,640]{1,0:T(8,128)(2,1)}), bf16[6144,640]{1,0:T(8,128)(2,1)}) %all-gather.17.cloned.1.call-update) | async-done | bytes 7864336 | tf_op jit(solution)/shard_map/all_gather | solution.py:94
  323.8 3.9 gather_fusion.1
  327.7 163.2 %while.18 = (s32[]{:T(128)}, f32[384,5]{0,1:T(8,128)S(1)}, f32[384,5]{0,1:T(8,128)S(1)}, f32[384,5,128]{0,2,1:T(8,128)}, s32[384]{0:T(512)S(1)}, /*index=5*/s32[...) while((s32[]{:T(128)}, f32[384,5]{0,1:T(8,128)S(1)}, ...), condition=%wide.region_12.13_spmd.clone, body=%wide.region_9.12_spmd.clone.sunk | while | flops 515073408 | bytes 20414148 | solution.py:135
  332.6 2.9 fusion.52
  337.0 4.0 fusion.54
  346.0 2.9 fusion.52
  350.4 4.3 fusion.54
  364.0 4.3 fusion.54
  377.6 4.3 fusion.54
  391.2 4.3 fusion.54
  404.8 4.3 fusion.54
  418.5 4.3 fusion.54
  432.1 4.3 fusion.54
  445.7 4.3 fusion.54
  459.3 4.3 fusion.54
  472.9 4.3 fusion.54
  486.6 4.3 fusion.54
  (179 shorter events, 134.5 us)
Async XLA Ops:
  7.2 76.0 %all-gather.7.cloned.1.call-start = ((), (), s32[]{:S(2)}) async-start(), calls=%async_computation | async-start | bytes 4423680 | tf_op jit(solution)/shard_map/all_gather | solution.py:66
  9.2 117.7 %all-gather.13.cloned.1.call-start = ((), (), s32[]{:S(2)}) async-start(), calls=%async_computation.3 | async-start | bytes 6963200 | tf_op jit(solution)/shard_map/all_gather | solution.py:74
  10.0 163.1 %all-gather.9.cloned.1.call-start = ((), (), s32[]{:S(2)}) async-start(), calls=%async_computation.1 | async-start | bytes 6963200 | tf_op jit(solution)/shard_map/all_gather | solution.py:75
  10.7 211.0 %all-gather.15.cloned.1.call-start = ((), (), s32[]{:S(2)}) async-start(), calls=%async_computation.4 | async-start | bytes 6963200 | tf_op jit(solution)/shard_map/all_gather | solution.py:76
  11.3 260.3 %all-gather.11.cloned.1.call-start = ((), (), s32[]{:S(2)}) async-start(), calls=%async_computation.2 | async-start | bytes 8355840 | tf_op jit(solution)/shard_map/all_gather | solution.py:93
  83.1 3.3 copy-start
  183.8 30.1 %copy-start.2 = (f32[5,64,2]{2,1,0:T(8,128)S(1)}, f32[5,64,2]{2,1,0:T(8,128)}, u32[]{:S(2)}) copy-start(f32[5,64,2]{2,1,0:T(8,128)} %mul.253) | copy-start | bytes 7684
  183.8 30.6 %copy-start.1 = (f32[5,64,2]{2,1,0:T(8,128)S(1)}, f32[5,64,2]{2,1,0:T(8,128)}, u32[]{:S(2)}) copy-start(f32[5,64,2]{2,1,0:T(8,128)} %mul.277) | copy-start | bytes 7684
  221.7 102.1 %all-gather.17.cloned.1.call-start = ((), (), s32[]{:S(2)}) async-start(), calls=%async_computation.5 | async-start | bytes 8355840 | tf_op jit(solution)/shard_map/all_gather | solution.py:94
  233.6 5.4 %copy-start.3 = (s32[48]{0:T(128)S(1)}, s32[48]{0:T(128)}, u32[]{:S(2)}) copy-start(s32[48]{0:T(128)} %param.21) | copy-start | bytes 580
Sparse Core Ops, SparseCore 0:
  10.9 72.1 all-gather.6
  84.8 42.0 all-gather.12
  128.7 44.3 all-gather.8
  174.6 44.7 all-gather.14
  221.8 49.8 all-gather.10
  273.2 50.5 all-gather.16
where the time goes:
time: 504 us; the launch traced here: 501 us
  waiting for transfers between devices  204 us (40%)
  matrix products  118 us (23%)
  local copies, waits for them, and re-layouts  72.7 us (14%)
  other arithmetic  70.4 us (14%)
  blocking collectives  20.8 us (4%)
  between operations  14.3 us (3%)
    all_gather x1, waiting for transfers between devices, body(): full_rows = lax.all_gather(hidden, 'col', axis=1, tiled=True)  66 us
    dot_general x12, matrix products, attend_block(): jnp.einsum('qhk,khd->qhd', weights.astype(jnp.bfloat16), value_tile, pref...  51.2 us
    all_gather x1, waiting for transfers between devices, body(): lax.all_gather(value, 'row', axis=0, tiled=True)  37.5 us
    all_gather x1, waiting for transfers between devices, body(): lax.all_gather(w_query, 'row', axis=0, tiled=True)  35.4 us
    reduce_sum x12, other arithmetic, attend_block(): totals = totals * factor + jnp.sum(weights, axis=2)  35.3 us
    dot_general x12, matrix products, attend_block(): jnp.einsum('qhd,khd->qhk', query_tile, key_tile, preferred_element_type=j...  34.4 us
    all_gather x1, waiting for transfers between devices, body(): lax.all_gather(w_key, 'row', axis=0, tiled=True)  34.3 us
    dot_general x3, matrix products, blockwise(): jnp.einsum('tnf,nfo->nto', columns, weight_blocks, preferred_element_type...  32.5 us
  transfers between devices with their start and end apart: 6, of which 5 were waited for; matrix products, arithmetic and copies ran while one was open for 18% of the time, Pallas kernels for 0%

commit v1 on v0

v1 whole, which is shorter than its diff:
```python
import functools

import jax
import jax.numpy as jnp
from jax import lax
from jax.experimental import pallas as pl
from jax.experimental.pallas import tpu as pltpu
from jax.sharding import PartitionSpec as P

HEAD_DIM = 128
PAGE = 128
KEY_BLOCK = 512
LOG2E = 1.4426950408889634
epsilon = 1e-06


def rotary_table(positions, pair_count):
    frame_pairs = pair_count - 2 * (pair_count // 3)
    side_pairs = pair_count // 3
    column = jnp.arange(pair_count)
    frame_rate = 10000.0 ** (-column.astype(jnp.float32) / frame_pairs)
    height_rate = 10000.0 ** (-(column - frame_pairs).astype(jnp.float32) / side_pairs)
    width_rate = 10000.0 ** (-(column - frame_pairs - side_pairs).astype(jnp.float32) / side_pairs)
    coords = positions.astype(jnp.float32)
    angles = jnp.where(
        column < frame_pairs,
        coords[0][:, None] * frame_rate,
        jnp.where(
            column < frame_pairs + side_pairs,
            coords[1][:, None] * height_rate,
            coords[2][:, None] * width_rate,
        ),
    )
    return (jnp.cos(angles), jnp.sin(angles))


def rotate(values, cosine, sine_table, head_dim):
    row_count = values.shape[0]
    head_count = values.shape[1] // head_dim
    paired = values.reshape(row_count, head_count, head_dim // 2, 2)
    former = paired[..., 0]
    latter = paired[..., 1]
    cosine = cosine[:, None, :]
    sine_table = sine_table[:, None, :]
    turned = jnp.stack(
        [former * cosine - latter * sine_table, former * sine_table + latter * cosine], axis=-1
    )
    return turned.reshape(row_count, head_count * head_dim)


def modulate(activations, modulation):
    average = jnp.mean(activations, axis=1, keepdims=True)
    centred = activations - average
    variance = jnp.mean(centred * centred, axis=1, keepdims=True)
    normed = centred * lax.rsqrt(variance + epsilon)
    return (normed * (1.0 + modulation[1]) + modulation[0]).astype(jnp.bfloat16)


def attend_kernel(
    plan, query, keys, values, query_segs, key_segs, attended, pages,
    key_buf, value_buf, top, acc, load_sem, page_sem,
):
    rows, width = query.shape
    heads = width // HEAD_DIM
    block = KEY_BLOCK
    own_pages = pages.shape[1]
    lo, hi = plan[0], plan[1]

    def page_copy(which, j):
        source = (keys, values)[which]
        start = pl.multiple_of(plan[2 + j] * PAGE, PAGE)
        return pltpu.make_async_copy(
            source.at[pl.ds(start, PAGE)], pages.at[which, j], page_sem.at[which, j]
        )

    def load(number, slot):
        start = pl.multiple_of(number * block, block)
        return (
            pltpu.make_async_copy(
                keys.at[pl.ds(start, block)], key_buf.at[slot], load_sem.at[0, slot]
            ),
            pltpu.make_async_copy(
                values.at[pl.ds(start, block)], value_buf.at[slot], load_sem.at[1, slot]
            ),
        )

    for copy in load(lo, 0):
        copy.start()
    for which in range(2):
        for j in range(own_pages):
            page_copy(which, j).start()
    top[...] = jnp.full_like(top, -1e30)
    acc[...] = jnp.zeros_like(acc)
    ones = jnp.ones((block, HEAD_DIM), jnp.bfloat16)
    scale = HEAD_DIM ** (-0.5) * LOG2E

    @pl.loop(lo, hi)
    def _(number):
        slot = lax.rem(number - lo, 2)
        for copy in load(number, slot):
            copy.wait()

        @pl.when(number + 1 < hi)
        def _():
            for copy in load(number + 1, 1 - slot):
                copy.start()

        allowed = query_segs[:, 0:1] == key_segs[number]
        for h in range(heads):
            part = pl.ds(h * HEAD_DIM, HEAD_DIM)
            scores = lax.dot_general(
                query[:, part], key_buf[slot, :, part], (((1,), (1,)), ((), ())),
                preferred_element_type=jnp.float32,
            ) * scale
            scores = jnp.where(allowed, scores, -1e30)
            old = top[h]
            new = jnp.maximum(old, jnp.max(scores, axis=1, keepdims=True))
            top[h] = new
            weights = jnp.where(allowed, jnp.exp2(scores - new[:, 0:1]), 0.0)
            factor = jnp.exp2(old - new)
            mixed = jnp.dot(
                weights.astype(jnp.bfloat16),
                jnp.concatenate([value_buf[slot, :, part], ones], axis=1),
                preferred_element_type=jnp.float32,
            )
            acc[h] = acc[h] * jnp.concatenate([factor, factor], axis=1) + mixed

    for h in range(heads):
        part = pl.ds(h * HEAD_DIM, HEAD_DIM)
        attended[:, part] = (acc[h, :, :HEAD_DIM] / acc[h, :, HEAD_DIM:]).astype(attended.dtype)
    for which in range(2):
        for j in range(own_pages):
            page_copy(which, j).wait()


def attend(query, keys, values, segment_ids, page_table):
    rows, width = query.shape
    heads = width // HEAD_DIM
    tokens = keys.shape[0]
    row = lax.axis_index("row")
    query_segs = lax.dynamic_slice_in_dim(segment_ids, row * rows, rows, 0)
    first, last = query_segs[0], query_segs[-1]
    lo = jnp.sum(segment_ids < first) // KEY_BLOCK
    hi = (jnp.sum(segment_ids <= last) + KEY_BLOCK - 1) // KEY_BLOCK
    own_pages = rows // PAGE
    slots = row * own_pages + jnp.arange(own_pages)
    numbers = jnp.arange(page_table.shape[0], dtype=jnp.int32)
    owned = jnp.sum(jnp.where(page_table[None] == slots[:, None], numbers[None], 0), axis=1)
    plan = jnp.concatenate([jnp.stack([lo, hi]).astype(jnp.int32), owned.astype(jnp.int32)])
    any_spec = pl.BlockSpec(memory_space=pl.ANY)
    vmem = pl.BlockSpec(memory_space=pltpu.VMEM)
    return pl.pallas_call(
        attend_kernel,
        out_shape=(
            jax.ShapeDtypeStruct((rows, width), jnp.bfloat16),
            jax.ShapeDtypeStruct((2, own_pages, PAGE, width), jnp.bfloat16),
        ),
        in_specs=[
            pl.BlockSpec(memory_space=pltpu.SMEM), vmem, any_spec, any_spec, vmem, vmem,
        ],
        out_specs=(vmem, any_spec),
        scratch_shapes=[
            pltpu.VMEM((2, KEY_BLOCK, width), jnp.bfloat16),
            pltpu.VMEM((2, KEY_BLOCK, width), jnp.bfloat16),
            pltpu.VMEM((heads, rows, HEAD_DIM), jnp.float32),
            pltpu.VMEM((heads, rows, 2 * HEAD_DIM), jnp.float32),
            pltpu.SemaphoreType.DMA((2, 2)),
            pltpu.SemaphoreType.DMA((2, own_pages)),
        ],
        compiler_params=pltpu.CompilerParams(vmem_limit_bytes=40 * 2**20),
        name="attend",
    )(
        plan, query, keys, values, query_segs[:, None],
        segment_ids.reshape(tokens // KEY_BLOCK, 1, KEY_BLOCK),
    )


def body(
    hidden, modulation, w_query, w_key, w_value, q_gain, k_gain, positions, segment_ids, page_table
):
    w_query, w_key, w_value = (
        lax.all_gather(w, "row", axis=0, tiled=True) for w in (w_query, w_key, w_value)
    )
    full_rows = lax.all_gather(hidden, "col", axis=1, tiled=True)
    modulated = modulate(full_rows.astype(jnp.float32), modulation)
    full_width = full_rows.shape[1]
    query_raw, key_raw, value_raw = (
        jnp.dot(modulated, w, preferred_element_type=jnp.float32)
        for w in (w_query, w_key, w_value)
    )
    squares = lax.psum(
        (jnp.sum(query_raw * query_raw, axis=1), jnp.sum(key_raw * key_raw, axis=1)), "col"
    )
    query_normed = query_raw * lax.rsqrt(squares[0][:, None] / full_width + epsilon) * q_gain
    key_normed = key_raw * lax.rsqrt(squares[1][:, None] / full_width + epsilon) * k_gain
    cosine, sine_table = rotary_table(positions, HEAD_DIM // 2)
    query = rotate(query_normed, cosine, sine_table, HEAD_DIM).astype(jnp.bfloat16)
    key = rotate(key_normed, cosine, sine_table, HEAD_DIM).astype(jnp.bfloat16)
    value = value_raw.astype(jnp.bfloat16)
    keys_all = lax.all_gather(key, "row", axis=0, tiled=True)
    values_all = lax.all_gather(value, "row", axis=0, tiled=True)
    return attend(query, keys_all, values_all, segment_ids, page_table)


def solution(mesh):
    in_specs = (
        P("row", "col"),
        P(),
        P("row", "col"),
        P("row", "col"),
        P("row", "col"),
        P("col"),
        P("col"),
        P(None, "row"),
        P(),
        P(),
    )
    out_specs = (P("row", "col"), P(None, "row", None, "col"))
    return jax.shard_map(body, mesh=mesh, in_specs=in_specs, out_specs=out_specs, check_vma=False)
```

time: 504 us -> 353 us (0.70)
  matrix products: 118 us -> 23.6 us
  local copies, waits for them, and re-layouts: 72.7 us -> 8.02 us
  other arithmetic: 70.4 us -> 18.8 us
  waiting for transfers between devices: 204 us -> 245 us
  Pallas kernels: 0 us -> 18.2 us
    dot_general x27 -> x3, matrix products: 118 us -> 23.6 us  [body(): jnp.dot(modulated, w, preferred_element_type=jnp.float32)]
    reduce_sum x17 -> x2, other arithmetic: 47 us -> 2.22 us  [the longest x1 2.04 us: attend(): lo = jnp.sum(segment_ids < first) // KEY_BLOCK]
    dynamic_slice x49 -> x1, local copies, waits for them, and re-layouts: 40.4 us -> 0.08 us  [attend(): query_segs = lax.dynamic_slice_in_dim(segment_ids, row * rows, rows, 0)]
    all_gather x5, waiting for transfers between devices: 136 us -> 172 us  [the longest x3 82.9 us: body(): lax.all_gather(w, 'row', axis=0, tiled=True)]
    pallas_call x0 -> x1, Pallas kernels: none -> 18.2 us  [attend(): pl.pallas_call(attend_kernel, out_shape=(jax.ShapeDtypeStruct((rows, widt...]
    all_gather x1 -> x0, local copies, waits for them, and re-layouts: 10.4 us -> none  [body(): lax.all_gather(key, 'row', axis=0, tiled=True)]
    gather x2 -> x0, local copies, waits for them, and re-layouts: 8.06 us -> none  [the longest x1 4.19 us: body(): key_pages = keys_all.reshape(page_count, PAGE, local_cols)[owned]]
  transfers between devices with their start and end apart: 6 -> 6, of which waited for: 5 -> 6; matrix products, arithmetic and copies ran while one was open for 18% -> 13% of each run, Pallas kernels for 0% -> 0%
where the time goes in v1:
time: 353 us; the launch traced here: 352 us
  waiting for transfers between devices  245 us (69%)
  matrix products  23.6 us (7%)
  blocking collectives  20.9 us (6%)
  other arithmetic  18.8 us (5%)
  Pallas kernels  18.2 us (5%)
  between operations  17.6 us (5%)
  local copies, waits for them, and re-layouts  8.02 us (2%)
    all_gather x3, waiting for transfers between devices, body(): lax.all_gather(w, 'row', axis=0, tiled=True)  82.9 us
    all_gather x1, waiting for transfers between devices, body(): full_rows = lax.all_gather(hidden, 'col', axis=1, tiled=True)  70.5 us
    all_gather x1, waiting for transfers between devices, body(): values_all = lax.all_gather(value, 'row', axis=0, tiled=True)  52.7 us
    all_gather x1, waiting for transfers between devices, body(): keys_all = lax.all_gather(key, 'row', axis=0, tiled=True)  36.3 us
    dot_general x3, matrix products, body(): jnp.dot(modulated, w, preferred_element_type=jnp.float32)  23.6 us
    psum x1, blocking collectives, body(): lax.psum((jnp.sum(query_raw * query_raw, axis=1), jnp.sum(key_raw * key_r...  20.9 us
    pallas_call x1, Pallas kernels, attend(): pl.pallas_call(attend_kernel, out_shape=(jax.ShapeDtypeStruct((rows, widt...  18.2 us
  transfers between devices with their start and end apart: 6, of which 6 were waited for; matrix products, arithmetic and copies ran while one was open for 13% of the time, Pallas kernels for 0%

profile of v1, /device:TPU:1, one launch (start us, length us, event | category | flops | bytes accessed | tf_op | source)
XLA Modules:
  0.0 352.2 jit_solution(13674548842379225608)
XLA Ops:
  7.2 0.7 all-gather.7.cloned.1.call-update
  7.9 0.7 all-gather.9.cloned.1.call-update
  8.7 0.7 all-gather.11.cloned.1.call-update
  9.4 0.5 all-gather.15.cloned.1.call-update
  10.0 0.7 convert_element_type.50
  10.8 0.5 fusion.7
  11.2 0.9 slice_add_fusion
  12.1 70.5 %all-gather.7.cloned.1.call-done = bf16[384,5120]{1,0:T(8,128)(2,1)} async-done(((bf16[384,640]{1,0:T(8,128)(2,1)}), bf16[384,5120]{1,0:T(8,128)(2,1)}) %all-gather.7.cloned.1.call-update) | async-done | bytes 3932176 | tf_op jit(solution)/shard_map/all_gather | solution.py:184
  82.7 2.9 convert_reduce_fusion
  85.5 0.4 copy-done.2
  85.9 1.2 fusion.2
  87.1 4.0 %fusion.5 = bf16[384,5120]{1,0:T(8,128)(2,1)} fusion(bf16[384,5120]{1,0:T(8,128)(2,1)S(1)} %copy-done.2, f32[5120]{0:T(1024)S(1)} %bitcast.23, f32[5120]{0:T(1024)S(1)} %bitcast.22, f32[384]{0:T(512)S(1)} %add_rsqrt_fusion.2, f32[384]{0:T(512)S(1)} %broadcast_multiply_fusion), kind=kLoop, calls=%fused_computation.7 | loop fusion | flops 11796480 | bytes 7908352 | tf_op jit(solution)/shard_map/convert_element_type | solution.py:56
  91.1 35.4 %all-gather.9.cloned.1.call-done = bf16[5120,640]{1,0:T(8,128)(2,1)} async-done(((bf16[320,640]{1,0:T(8,128)(2,1)}), bf16[5120,640]{1,0:T(8,128)(2,1)}) %all-gather.9.cloned.1.call-update) | async-done | bytes 6553616 | tf_op jit(solution)/shard_map/all_gather | solution.py:182
  126.5 7.3 %multiply_reduce_fusion.1 = (f32[384]{0:T(512)S(1)}, f32[384,640]{1,0:T(8,128)S(1)}) fusion(bf16[384,5120]{1,0:T(8,128)(2,1)} %fusion.5, bf16[5120,640]{1,0:T(8,128)(2,1)} %all-gather.9.cloned.1.call-done), kind=kOutput, calls=%fused_computation.12 | convolution fusion | flops 2517073408 | bytes 11470336 | tf_op jit(solution)/shard_map/dot_general | solution.py:188
  133.8 38.8 %all-gather.11.cloned.1.call-done = bf16[5120,640]{1,0:T(8,128)(2,1)} async-done(((bf16[320,640]{1,0:T(8,128)(2,1)}), bf16[5120,640]{1,0:T(8,128)(2,1)}) %all-gather.11.cloned.1.call-update) | async-done | bytes 6553616 | tf_op jit(solution)/shard_map/all_gather | solution.py:182
  172.6 8.2 %multiply_reduce_fusion = (f32[384]{0:T(512)S(1)}, f32[384,640]{1,0:T(8,128)}) fusion(bf16[384,5120]{1,0:T(8,128)(2,1)} %fusion.5, bf16[5120,640]{1,0:T(8,128)(2,1)} %all-gather.11.cloned.1.call-done), kind=kOutput, calls=%fused_computation.10 | convolution fusion | flops 2517073408 | bytes 11470336 | tf_op jit(solution)/shard_map/dot_general | solution.py:188
  180.8 20.9 %all-reduce = (f32[384]{0:T(512)S(1)}, f32[384]{0:T(512)S(1)}) all-reduce(f32[384]{0:T(512)S(1)} %get-tuple-element.21, f32[384]{0:T(512)S(1)} %get-tuple-element.23), channel_id=1, replica_groups=mesh['row'=16,'col'=8] {'col'}, use_global_device_ids=true, to_apply=%region_6.7 | all-reduce | flops 768 | bytes 6144 | tf_op jit(solution)/shard_map/psum | solution.py:191
  202.2 0.6 reshape.257
  202.8 1.4 multiply_multiply_fusion
  204.5 0.6 reshape.258
  205.1 2.6 subtract_convert_fusion
  207.7 1.1 pad_maximum_fusion.1
  209.0 1.0 copy.19
  210.1 8.8 %all-gather.15.cloned.1.call-done = bf16[5120,640]{1,0:T(8,128)(2,1)} async-done(((bf16[320,640]{1,0:T(8,128)(2,1)}), bf16[5120,640]{1,0:T(8,128)(2,1)}) %all-gather.15.cloned.1.call-update) | async-done | bytes 6553616 | tf_op jit(solution)/shard_map/all_gather | solution.py:182
  218.9 8.0 %convolution_convert_fusion = bf16[384,640]{1,0:T(8,128)(2,1)} fusion(bf16[384,5120]{1,0:T(8,128)(2,1)} %fusion.5, bf16[5120,640]{1,0:T(8,128)(2,1)} %all-gather.15.cloned.1.call-done), kind=kOutput, calls=%fused_computation.8 | convolution fusion | flops 2516828160 | bytes 10977280 | tf_op jit(solution)/shard_map/dot_general | solution.py:188
  227.0 0.7 fusion.8
  227.7 2.0 convert_reduce_fusion.2
  233.4 1.1 pad_maximum_fusion
  235.0 36.3 %all-gather.13.cloned.1.call-done.keys = bf16[6144,640]{1,0:T(8,128)(2,1)} async-done(((bf16[384,640]{1,0:T(8,128)(2,1)}), bf16[6144,640]{1,0:T(8,128)(2,1)}) %all-gather.13.cloned.1.call-update) | async-done | bytes 7864336 | tf_op jit(solution)/shard_map/all_gather | solution.py:200
  271.2 52.7 %all-gather.17.cloned.1.call-done.values = bf16[6144,640]{1,0:T(8,128)(2,1)} async-done(((bf16[384,640]{1,0:T(8,128)(2,1)}), bf16[6144,640]{1,0:T(8,128)(2,1)}) %all-gather.17.cloned.1.call-update) | async-done | bytes 7864336 | tf_op jit(solution)/shard_map/all_gather | solution.py:201
  323.9 3.2 copy-done
  327.2 18.2 %attend.1 = (bf16[384,640]{1,0:T(8,128)(2,1)}, bf16[2,3,128,640]{3,2,1,0:T(8,128)(2,1)}) custom-call(s32[5]{0:T(128)S(1)} %pad_add_fusion.plan, bf16[384,640]{1,0:T(8,128)(2,1)S(1)} %copy.20.query, bf16[6144,640]{1,0:T(8,128)(2,1)S(1)} %copy-done, bf16[6144,640]{1,0:T(8,128)(2,1)} %all-gather.17.cloned.1.call-done.values, ...), custom_call_target="tpu_custom_call" | custom-call | tf_op jit(solution)/shard_map/attend/pallas_call | solution.py:152
  (36 shorter events, 2.3 us)
Async XLA Ops:
  7.2 75.5 %all-gather.7.cloned.1.call-start = ((), (), s32[]{:S(2)}) async-start(), calls=%async_computation | async-start | bytes 4423680 | tf_op jit(solution)/shard_map/all_gather | solution.py:184
  7.9 118.6 %all-gather.9.cloned.1.call-start = ((), (), s32[]{:S(2)}) async-start(), calls=%async_computation.1 | async-start | bytes 6963200 | tf_op jit(solution)/shard_map/all_gather | solution.py:182
  8.6 163.9 %all-gather.11.cloned.1.call-start = ((), (), s32[]{:S(2)}) async-start(), calls=%async_computation.2 | async-start | bytes 6963200 | tf_op jit(solution)/shard_map/all_gather | solution.py:182
  9.4 209.5 %all-gather.15.cloned.1.call-start = ((), (), s32[]{:S(2)}) async-start(), calls=%async_computation.4 | async-start | bytes 6963200 | tf_op jit(solution)/shard_map/all_gather | solution.py:182
  10.0 261.3 %all-gather.13.cloned.1.call-start = ((), (), s32[]{:S(2)}) async-start(), calls=%async_computation.3 | async-start | bytes 8355840 | tf_op jit(solution)/shard_map/all_gather | solution.py:200
  82.7 3.3 copy-start.2
  133.8 67.9 %copy-start.3 = (f32[640]{0:T(1024)S(1)}, f32[640]{0:T(1024)}, u32[]{:S(2)}) copy-start(f32[640]{0:T(1024)} %param.15) | copy-start | bytes 7684
  133.8 69.0 %copy-start.4 = (f32[640]{0:T(1024)S(1)}, f32[640]{0:T(1024)}, u32[]{:S(2)}) copy-start(f32[640]{0:T(1024)} %param.16) | copy-start | bytes 7684
  210.0 16.9 %copy-start.1 = (s32[6144]{0:T(1024)S(1)}, s32[6144]{0:T(1024)}, u32[]{:S(2)}) copy-start(s32[6144]{0:T(1024)} %param.18) | copy-start | bytes 73732
  210.0 23.1 %copy-start.5 = (s32[48]{0:T(128)S(1)}, s32[48]{0:T(128)}, u32[]{:S(2)}) copy-start(s32[48]{0:T(128)} %param.19) | copy-start | bytes 580
  210.1 113.9 %all-gather.17.cloned.1.call-start = ((), (), s32[]{:S(2)}) async-start(), calls=%async_computation.5 | async-start | bytes 8355840 | tf_op jit(solution)/shard_map/all_gather | solution.py:201
  323.9 3.2 copy-start
Sparse Core Ops, SparseCore 0:
  10.3 72.2 all-gather.6
  84.4 42.0 all-gather.8
  128.2 44.3 all-gather.10
  174.1 44.7 all-gather.14
  221.0 50.1 all-gather.12
  273.4 50.5 all-gather.16

commit v2 on v1

--- a/solution.py
+++ b/solution.py
@@ -1,7 +1,6 @@
-import functools
-
 import jax
 import jax.numpy as jnp
+import numpy as np
 from jax import lax
 from jax.experimental import pallas as pl
 from jax.experimental.pallas import tpu as pltpu
@@ -14,46 +13,362 @@
 epsilon = 1e-06
 
 
-def rotary_table(positions, pair_count):
+def rotary_rates(pair_count):
     frame_pairs = pair_count - 2 * (pair_count // 3)
     side_pairs = pair_count // 3
-    column = jnp.arange(pair_count)
-    frame_rate = 10000.0 ** (-column.astype(jnp.float32) / frame_pairs)
-    height_rate = 10000.0 ** (-(column - frame_pairs).astype(jnp.float32) / side_pairs)
-    width_rate = 10000.0 ** (-(column - frame_pairs - side_pairs).astype(jnp.float32) / side_pairs)
-    coords = positions.astype(jnp.float32)
-    angles = jnp.where(
-        column < frame_pairs,
-        coords[0][:, None] * frame_rate,
-        jnp.where(
-            column < frame_pairs + side_pairs,
-            coords[1][:, None] * height_rate,
-            coords[2][:, None] * width_rate,
+    column = np.arange(pair_count)
+    starts = [0, frame_pairs, frame_pairs + side_pairs, pair_count]
+    rates = np.zeros((8, 2 * pair_count), np.float32)
+    for i in range(3):
+        count = starts[i + 1] - starts[i]
+        rate = np.power(10000.0, -(column - starts[i]) / count).astype(np.float32)
+        inside = (column >= starts[i]) & (column < starts[i + 1])
+        rates[i] = np.repeat(np.where(inside, rate, 0.0), 2)
+    return rates
+
+
+class Ring:
+    def __init__(self, net, name, own, buffer, pair_first, sibling):
+        self.net, self.name, self.own, self.buffer = net, name, own, buffer
+        self.pair_first, self.sibling = pair_first, sibling
+
+    def view(self, pair, step, half=None, other=False):
+        return self.buffer(self.net.slot(self.name, pair, step, other), half)
+
+    def put(self, source, target, kind, link):
+        self.net.put(source, target, (self.name, kind), self.net.device(self.name, link))
+
+    def got(self, kind, view):
+        self.net.got(view, (self.name, kind))
+
+    def start(self):
+        mine = self.view(0, 0)
+        if self.pair_first:
+            self.put(self.own, mine, "p", "pair")
+        self.put(self.own, mine, "m", "up")
+        self.put(self.own, mine, "n", "down")
+        if not self.pair_first:
+            self.put(self.own, mine, "p", "pair")
+        if self.sibling:
+            self.put(self.own, mine, "so", "core")
+        self.net.local(self.own, mine)
+
+    def share(self, kind, view):
+        if self.sibling:
+            self.put(view, view, "s" + kind, "core")
+
+    def events(self):
+        def pair():
+            view = self.view(1, 0)
+            self.got("p", view)
+            if self.pair_first:
+                self.put(view, view, "pm", "up")
+                self.put(view, view, "pn", "down")
+            self.share("p", view)
+
+        def ring(prefix, where, direction):
+            def run():
+                step, kind, half, link = (
+                    (-1, "m", 0, "up") if direction == 0 else (1, "n", 1, "down")
+                )
+                view = self.view(where, step)
+                self.got(prefix + kind, view)
+                if where == 0 or self.pair_first:
+                    part = self.view(where, step, half)
+                    self.put(part, part, prefix + ("a", "b")[direction], link)
+                if where == 0 and not self.pair_first:
+                    self.put(view, view, "p" + kind, "pair")
+                self.share(prefix + kind, view)
+
+            return run
+
+        def far(prefix, where):
+            def run():
+                view = self.view(where, 2)
+                if where == 0 or self.pair_first:
+                    for half, kind in enumerate("ab"):
+                        self.got(prefix + kind, self.view(where, 2, half))
+                else:
+                    self.got(prefix + "f", view)
+                if where == 0 and not self.pair_first:
+                    self.put(view, view, "pf", "pair")
+                self.share(prefix + "f", view)
+
+            return run
+
+        near = [ring("", 0, 0), ring("", 0, 1)]
+        crossed = [ring("p", 1, 0), ring("p", 1, 1)]
+        if self.pair_first:
+            return [pair, *near, *crossed, far("", 0), far("p", 1)]
+        return [*near, pair, far("", 0), *crossed, far("p", 1)]
+
+    def finish(self):
+        if self.sibling:
+            self.got("so", self.view(0, 0, other=True))
+            for prefix, where in (("", 0), ("p", 1)):
+                self.got("s" + prefix + "m", self.view(where, -1, other=True))
+                self.got("s" + prefix + "n", self.view(where, 1, other=True))
+                self.got("s" + prefix + "f", self.view(where, 2, other=True))
+            self.got("sp", self.view(1, 0, other=True))
+
+
+class Net:
+    def __init__(self, send, recv, own_sem):
+        self.send, self.recv, self.own_sem = send, recv, own_sem
+        self.sent, self.kinds, self.locals = [], {}, []
+        row, col = lax.axis_index("row"), lax.axis_index("col")
+        self.row, self.col = row, col
+        self.core, self.y, self.z_lo = row % 2, (row // 2) % 4, row // 8
+        self.x, self.z_hi = col % 4, col // 4
+
+    def row_at(self, pair, step, other):
+        z_lo = 1 - self.z_lo if pair else self.z_lo
+        core = 1 - self.core if other else self.core
+        return z_lo * 8 + ((self.y + step + 4) % 4) * 2 + core
+
+    def col_at(self, pair, step):
+        z_hi = 1 - self.z_hi if pair else self.z_hi
+        return z_hi * 4 + (self.x + step + 4) % 4
+
+    def slot(self, name, pair, step, other):
+        return self.col_at(pair, step) if name == "x" else self.row_at(pair, step, other)
+
+    def device(self, name, link):
+        pair, step = {"pair": (1, 0), "up": (0, 1), "down": (0, -1), "core": (0, 0)}[link]
+        if name == "x":
+            return (self.row, self.col_at(pair, step))
+        return (self.row_at(pair, step, link == "core"), self.col)
+
+    def partners(self):
+        rows = [self.device("w", link) for link in ("pair", "up", "down", "core")]
+        return rows + self.peers()
+
+    def peers(self):
+        others = [(p, s) for p in (0, 1) for s in range(4) if (p, s) != (0, 0)]
+        return [(self.row, self.col_at(*o)) for o in others]
+
+    def number(self, kind):
+        return self.kinds.setdefault(kind, len(self.kinds))
+
+    def copy(self, source, target, kind, device):
+        return pltpu.make_async_remote_copy(
+            src_ref=source,
+            dst_ref=target,
+            send_sem=self.send.at[len(self.sent)],
+            recv_sem=self.recv.at[self.number(kind)],
+            device_id=device,
+            device_id_type=pl.DeviceIdType.MESH,
+        )
+
+    def put(self, source, target, kind, device):
+        copy = self.copy(source, target, kind, device)
+        copy.start()
+        self.sent.append(copy)
+
+    def got(self, view, kind):
+        pltpu.make_async_remote_copy(
+            src_ref=view,
+            dst_ref=view,
+            send_sem=self.send.at[0],
+            recv_sem=self.recv.at[self.number(kind)],
+            device_id=self.device("w", "core"),
+            device_id_type=pl.DeviceIdType.MESH,
+        ).wait_recv()
+
+    def local(self, source, target):
+        copy = pltpu.make_async_copy(source, target, self.own_sem.at[len(self.locals)])
+        copy.start()
+        self.locals.append(copy)
+
+
+def project_kernel(
+    hidden, modulation, w_query, w_key, w_value, q_gain, k_gain, places, rates,
+    query_out, keys_all, values_all,
+    hidden_all, modulated, weights, raw, key_own, value_own, squares, tables,
+    send, recv, own_sem,
+):
+    net = Net(send, recv, own_sem)
+    rows, width = hidden.shape
+    deep = w_query.shape[0]
+    features = modulation.shape[1]
+    heads = width // HEAD_DIM
+
+    barrier = pltpu.get_barrier_semaphore()
+    partners = net.partners()
+    for device in partners:
+        pl.semaphore_signal(
+            barrier, inc=1, device_id=device, device_id_type=pl.DeviceIdType.MESH
+        )
+    pl.semaphore_wait(barrier, len(partners))
+
+    def cut(start, size, half):
+        if half is None:
+            return pl.ds(pl.multiple_of(start, 16), size)
+        return pl.ds(pl.multiple_of(start + half * (size // 2), 16), size // 2)
+
+    def weight_view(which):
+        return lambda slot, half: weights.at[which, cut(slot * deep, deep, half)]
+
+    def token_view(ref):
+        return lambda slot, half: ref.at[slot, cut(0, rows, half)]
+
+    hid = Ring(net, "x", hidden, token_view(hidden_all), True, False)
+    wk = Ring(net, "wk", w_key, weight_view(1), True, True)
+    wv = Ring(net, "wv", w_value, weight_view(2), False, True)
+    wq = Ring(net, "wq", w_query, weight_view(0), True, True)
+    kk = Ring(net, "kk", key_own, token_view(keys_all), True, True)
+    vv = Ring(net, "vv", value_own, token_view(values_all), False, True)
+
+    def pull(*queues):
+        queues = [list(q) for q in queues]
+        while any(queues):
+            for q in queues:
+                if q:
+                    q.pop(0)()
+
+    hid.start()
+    wv.start()
+    wk.start()
+
+    angle = (
+        places[:, 0:1] * rates[0:1] + places[:, 1:2] * rates[1:2] + places[:, 2:3] * rates[2:3]
+    )
+    lane = lax.broadcasted_iota(jnp.int32, angle.shape, 1)
+    even = lane % 2 == 0
+    tables[0] = jnp.cos(angle)
+    sine = jnp.sin(angle)
+    tables[1] = jnp.where(even, -sine, sine)
+
+    def normalise():
+        net.locals[0].wait()
+        groups = hidden_all.shape[0]
+
+        def add(g, total):
+            return total + jnp.sum(hidden_all[g].astype(jnp.float32), axis=1, keepdims=True)
+
+        zero = jnp.zeros((rows, 1), jnp.float32)
+        average = lax.fori_loop(0, groups, add, zero) / features
+
+        def spread(g, total):
+            centred = hidden_all[g].astype(jnp.float32) - average
+            return total + jnp.sum(centred * centred, axis=1, keepdims=True)
+
+        variance = lax.fori_loop(0, groups, spread, zero) / features
+        scale = lax.rsqrt(variance + epsilon)
+
+        @pl.loop(0, groups)
+        def _(g):
+            part = pl.ds(pl.multiple_of(g * width, width), width)
+            normed = (hidden_all[g].astype(jnp.float32) - average) * scale
+            shifted = normed * (1.0 + modulation[1:2, part]) + modulation[0:1, part]
+            modulated[:, part] = shifted.astype(jnp.bfloat16)
+
+    def project(which):
+        step = 2 * width
+        raw[...] = jnp.zeros_like(raw)
+
+        @pl.loop(0, features // step)
+        def _(g):
+            part = pl.ds(pl.multiple_of(g * step, step), step)
+            raw[...] += jnp.dot(
+                modulated[:, part], weights[which, part, :], preferred_element_type=jnp.float32
+            )
+
+    def send_squares(number):
+        whole = raw[...]
+        part = jnp.zeros((rows, HEAD_DIM), jnp.float32)
+        for h in range(heads):
+            piece = whole[:, h * HEAD_DIM : (h + 1) * HEAD_DIM]
+            part = part + piece * piece
+        total = jnp.sum(part.T, axis=0, keepdims=True)
+        mine = squares.at[number, net.col]
+        squares[number, net.col] = jnp.broadcast_to(total, (8, rows))
+        for i, device in enumerate(net.peers()):
+            net.put(mine, mine, ("sq", number, i), device)
+
+    def turned(number, gain):
+        others = [(p, s) for p in (0, 1) for s in range(4) if (p, s) != (0, 0)]
+        for i, (pair, step) in enumerate(others):
+            net.got(squares.at[number, net.col_at(pair, -step)], ("sq", number, i))
+        total = jnp.sum(squares[number], axis=0)
+        column = jnp.broadcast_to(total[0:1], (HEAD_DIM, rows)).T
+        factor = lax.rsqrt(column / features + epsilon)
+        made = []
+        for h in range(heads):
+            part = slice(h * HEAD_DIM, (h + 1) * HEAD_DIM)
+            normed = raw[:, part] * factor * gain[0:1, part]
+            swapped = jnp.where(
+                even, pltpu.roll(normed, HEAD_DIM - 1, 1), pltpu.roll(normed, 1, 1)
+            )
+            made.append((normed * tables[0] + swapped * tables[1]).astype(jnp.bfloat16))
+        return jnp.concatenate(made, axis=1)
+
+    pull(wv.events(), wk.events(), hid.events())
+    wq.start()
+    normalise()
+    wv.finish()
+    for copy in net.locals[1:3]:
+        copy.wait()
+    project(2)
+    value_own[...] = raw[...].astype(jnp.bfloat16)
+    vv.start()
+    wk.finish()
+    project(1)
+    send_squares(0)
+    queue = wq.events()
+    for event in queue[:3]:
+        event()
+    key_own[...] = turned(0, k_gain)
+    kk.start()
+    pull(queue[3:], vv.events(), kk.events())
+    wq.finish()
+    net.locals[3].wait()
+    project(0)
+    send_squares(1)
+    query_out[...] = turned(1, q_gain)
+    vv.finish()
+    kk.finish()
+    for copy in net.locals[4:]:
+        copy.wait()
+    for copy in net.sent:
+        copy.wait_send()
+
+
+def project(hidden, modulation, w_query, w_key, w_value, q_gain, k_gain, positions):
+    rows, width = hidden.shape
+    deep = w_query.shape[0]
+    features = modulation.shape[1]
+    members, groups = features // deep, features // width
+    places = positions.astype(jnp.float32).T
+    any_spec = pl.BlockSpec(memory_space=pl.ANY)
+    vmem = pl.BlockSpec(memory_space=pltpu.VMEM)
+    tokens = jax.ShapeDtypeStruct((members, rows, width), jnp.bfloat16)
+    return pl.pallas_call(
+        project_kernel,
+        out_shape=(jax.ShapeDtypeStruct((rows, width), jnp.bfloat16), tokens, tokens),
+        in_specs=[vmem, vmem, any_spec, any_spec, any_spec, vmem, vmem, vmem, vmem],
+        out_specs=(vmem, any_spec, any_spec),
+        scratch_shapes=[
+            pltpu.VMEM((groups, rows, width), jnp.bfloat16),
+            pltpu.VMEM((rows, features), jnp.bfloat16),
+            pltpu.VMEM((3, features, width), jnp.bfloat16),
+            pltpu.VMEM((rows, width), jnp.float32),
+            pltpu.VMEM((rows, width), jnp.bfloat16),
+            pltpu.VMEM((rows, width), jnp.bfloat16),
+            pltpu.VMEM((2, groups, 8, rows), jnp.float32),
+            pltpu.VMEM((2, rows, HEAD_DIM), jnp.float32),
+            pltpu.SemaphoreType.DMA((128,)),
+            pltpu.SemaphoreType.DMA((128,)),
+            pltpu.SemaphoreType.DMA((6,)),
+        ],
+        compiler_params=pltpu.CompilerParams(
+            collective_id=0, has_side_effects=True, vmem_limit_bytes=56 * 2**20
         ),
+        name="project",
+    )(
+        hidden, modulation, w_query, w_key, w_value, q_gain[None], k_gain[None], places,
+        jnp.asarray(rotary_rates(HEAD_DIM // 2)),
     )
-    return (jnp.cos(angles), jnp.sin(angles))
-
-
-def rotate(values, cosine, sine_table, head_dim):
-    row_count = values.shape[0]
-    head_count = values.shape[1] // head_dim
-    paired = values.reshape(row_count, head_count, head_dim // 2, 2)
-    former = paired[..., 0]
-    latter = paired[..., 1]
-    cosine = cosine[:, None, :]
-    sine_table = sine_table[:, None, :]
-    turned = jnp.stack(
-        [former * cosine - latter * sine_table, former * sine_table + latter * cosine], axis=-1
-    )
-    return turned.reshape(row_count, head_count * head_dim)
-
-
-def modulate(activations, modulation):
-    average = jnp.mean(activations, axis=1, keepdims=True)
-    centred = activations - average
-    variance = jnp.mean(centred * centred, axis=1, keepdims=True)
-    normed = centred * lax.rsqrt(variance + epsilon)
-    return (normed * (1.0 + modulation[1]) + modulation[0]).astype(jnp.bfloat16)
 
 
 def attend_kernel(
@@ -178,28 +493,13 @@
 def body(
     hidden, modulation, w_query, w_key, w_value, q_gain, k_gain, positions, segment_ids, page_table
 ):
-    w_query, w_key, w_value = (
-        lax.all_gather(w, "row", axis=0, tiled=True) for w in (w_query, w_key, w_value)
+    query, keys, values = project(
+        hidden, modulation, w_query, w_key, w_value, q_gain, k_gain, positions
     )
-    full_rows = lax.all_gather(hidden, "col", axis=1, tiled=True)
-    modulated = modulate(full_rows.astype(jnp.float32), modulation)
-    full_width = full_rows.shape[1]
-    query_raw, key_raw, value_raw = (
-        jnp.dot(modulated, w, preferred_element_type=jnp.float32)
-        for w in (w_query, w_key, w_value)
+    tokens, width = segment_ids.shape[0], hidden.shape[1]
+    return attend(
+        query, keys.reshape(tokens, width), values.reshape(tokens, width), segment_ids, page_table
     )
-    squares = lax.psum(
-        (jnp.sum(query_raw * query_raw, axis=1), jnp.sum(key_raw * key_raw, axis=1)), "col"
-    )
-    query_normed = query_raw * lax.rsqrt(squares[0][:, None] / full_width + epsilon) * q_gain
-    key_normed = key_raw * lax.rsqrt(squares[1][:, None] / full_width + epsilon) * k_gain
-    cosine, sine_table = rotary_table(positions, HEAD_DIM // 2)
-    query = rotate(query_normed, cosine, sine_table, HEAD_DIM).astype(jnp.bfloat16)
-    key = rotate(key_normed, cosine, sine_table, HEAD_DIM).astype(jnp.bfloat16)
-    value = value_raw.astype(jnp.bfloat16)
-    keys_all = lax.all_gather(key, "row", axis=0, tiled=True)
-    values_all = lax.all_gather(value, "row", axis=0, tiled=True)
-    return attend(query, keys_all, values_all, segment_ids, page_table)
 
 
 def solution(mesh):

time: 353 us -> 191 us (0.54)
  waiting for transfers between devices: 245 us -> 0 us
  Pallas kernels: 18.2 us -> 171 us
  matrix products: 23.6 us -> 0 us
  blocking collectives: 20.9 us -> 0 us
  other arithmetic: 18.8 us -> 4.36 us
  between operations: 17.6 us -> 4.03 us
    all_gather x6 -> x0, waiting for transfers between devices: 242 us -> none  [the longest x3 82.9 us: body(): lax.all_gather(w, 'row', axis=0, tiled=True)]
    pallas_call x0 -> x1, Pallas kernels: none -> 150 us  [project(): pl.pallas_call(project_kernel, out_shape=(jax.ShapeDtypeStruct((rows, wid...]
    dot_general x3 -> x0, matrix products: 23.6 us -> none  [body(): jnp.dot(modulated, w, preferred_element_type=jnp.float32)]
    psum x1 -> x0, blocking collectives: 20.9 us -> none  [body(): lax.psum((jnp.sum(query_raw * query_raw, axis=1), jnp.sum(key_raw * key_r...]
    another operation x3 -> x0, other arithmetic: 4.82 us -> none
    reduce_sum x2 -> x0, other arithmetic: 4.03 us -> none  [the longest x1 2.86 us: modulate(): average = jnp.mean(activations, axis=1, keepdims=True)]
    convert_element_type x2 -> x1, other arithmetic: 4.67 us -> 0.69 us  [project(): places = positions.astype(jnp.float32).T]
  transfers between devices with their start and end apart: 6 -> 0, of which waited for: 6 -> 0; matrix products, arithmetic and copies ran while one was open for 13% -> 0% of each run, Pallas kernels for 0% -> 0%
where the time goes in v2:
time: 191 us; the launch traced here: 189 us
  Pallas kernels  171 us (90%)
  local copies, waits for them, and re-layouts  9.82 us (5%)
  other arithmetic  4.36 us (2%)
  between operations  4.03 us (2%)
    pallas_call x1, Pallas kernels, project(): pl.pallas_call(project_kernel, out_shape=(jax.ShapeDtypeStruct((rows, wid...  150 us
    pallas_call x1, Pallas kernels, attend(): pl.pallas_call(attend_kernel, out_shape=(jax.ShapeDtypeStruct((rows, widt...  20.4 us
    unnamed x6, local copies, waits for them, and re-layouts  4.99 us

profile of v2, /device:TPU:1, one launch (start us, length us, event | category | flops | bytes accessed | tf_op | source)
XLA Modules:
  0.0 188.8 jit_solution(8395579223512551159)
XLA Ops:
  0.6 0.8 select_reduce_fusion
  1.5 0.8 dynamic_slice.3
  2.3 0.6 fusion
  2.8 2.8 %convert_reduce_fusion.1 = (s32[]{:T(128)}, s32[]{:T(128)}) fusion(s32[6144]{0:T(1024)} %param.19, s32[]{:T(128)} %bitcast, s32[]{:T(128)} %bitcast.2), kind=kLoop, calls=%fused_computation.1 | loop fusion | flops 36862 | bytes 24592 | tf_op jit(solution)/shard_map/reduce_sum | solution.py:458
  9.0 0.1 pad_add_fusion.plan
  9.0 1.3 broadcast_in_dim.26.q_gain
  10.3 1.3 broadcast_in_dim.27.k_gain
  11.6 0.7 convert_element_type.11
  12.3 0.8 copy.16
  13.1 0.1 broadcast_in_dim.29.query_segs
  13.2 150.2 %project.1 = (bf16[384,640]{1,0:T(8,128)(2,1)}, bf16[16,384,640]{2,1,0:T(8,128)(2,1)}, bf16[16,384,640]{2,1,0:T(8,128)(2,1)}) custom-call(bf16[384,640]{1,0:T(8,128)(2,1)} %hidden.1, f32[2,5120]{1,0:T(2,128)} %modulation.1, bf16[320,640]{1,0:T(8,128)(2,1)} %w_query.1, bf16[320,640]{1,0:T(8,128)(2,1)} %w_key.1, bf16[320,640]{1,0:T(8,128)(2,1)} %w_value.1, ...), custom_call_target="tpu_custom_call" | custom-call | tf_op jit(solution)/shard_map/project/pallas_call | solution.py:346
  163.4 0.0 copy-start
  163.4 3.2 %copy-done = bf16[16,384,640]{2,1,0:T(8,128)(2,1)S(1)} copy-done((bf16[16,384,640]{2,1,0:T(8,128)(2,1)S(1)}, bf16[16,384,640]{2,1,0:T(8,128)(2,1)}, u32[]{:S(2)}) %copy-start) | copy-done | bytes 7864344
  166.6 0.0 copy-start.1
  166.6 1.0 copy-done.1
  167.7 0.0 copy-start.2
  167.7 0.7 copy-done.2
  168.4 20.4 %attend.1 = (bf16[384,640]{1,0:T(8,128)(2,1)}, bf16[2,3,128,640]{3,2,1,0:T(8,128)(2,1)}) custom-call(s32[5]{0:T(128)S(1)} %pad_add_fusion.plan, bf16[384,640]{1,0:T(8,128)(2,1)S(1)} %copy-done.1, bf16[6144,640]{1,0:T(8,128)(2,1)S(1)} %bitcast.8, bf16[6144,640]{1,0:T(8,128)(2,1)} %bitcast.10, s32[384,1]{1,0:T(8,128)S(1)} %broadcast_in_dim.29.query_segs, ...), custom_call_target="tpu_custom_call" | custom-call | tf_op jit(solution)/shard_map/attend/pallas_call | solution.py:467
  (1 shorter events, 0.0 us)
Async XLA Ops:
  163.4 3.2 %copy-start = (bf16[16,384,640]{2,1,0:T(8,128)(2,1)S(1)}, bf16[16,384,640]{2,1,0:T(8,128)(2,1)}, u32[]{:S(2)}) copy-start(bf16[16,384,640]{2,1,0:T(8,128)(2,1)} %get-tuple-element.6) | copy-start | bytes 23592964
  166.6 1.0 copy-start.1
  167.7 0.7 copy-start.2

commit v3 on v2

--- a/solution.py
+++ b/solution.py
@@ -8,7 +8,6 @@
 
 HEAD_DIM = 128
 PAGE = 128
-KEY_BLOCK = 512
 LOG2E = 1.4426950408889634
 epsilon = 1e-06
 
@@ -102,14 +101,15 @@
             return [pair, *near, *crossed, far("", 0), far("p", 1)]
         return [*near, pair, far("", 0), *crossed, far("p", 1)]
 
+    def met(self, pair, step):
+        kind = {0: "p" if pair else "o", -1: "m", 1: "n", 2: "f"}[step]
+        prefix = "p" if pair and step else ""
+        self.got("s" + prefix + kind, self.view(pair, step, other=True))
+
     def finish(self):
-        if self.sibling:
-            self.got("so", self.view(0, 0, other=True))
-            for prefix, where in (("", 0), ("p", 1)):
-                self.got("s" + prefix + "m", self.view(where, -1, other=True))
-                self.got("s" + prefix + "n", self.view(where, 1, other=True))
-                self.got("s" + prefix + "f", self.view(where, 2, other=True))
-            self.got("sp", self.view(1, 0, other=True))
+        for pair in (0, 1):
+            for step in (0, -1, 1, 2):
+                self.met(pair, step)
 
 
 class Net:
@@ -181,11 +181,12 @@
         self.locals.append(copy)
 
 
-def project_kernel(
-    hidden, modulation, w_query, w_key, w_value, q_gain, k_gain, places, rates,
-    query_out, keys_all, values_all,
+def attention_kernel(
+    hidden, modulation, w_query, w_key, w_value, q_gain, k_gain, positions, segs, rates,
+    attended, keys_all, values_all,
     hidden_all, modulated, weights, raw, key_own, value_own, squares, tables,
-    send, recv, own_sem,
+    query_own, marks, key_buf, value_buf, top, acc,
+    send, recv, own_sem, load_sem,
 ):
     net = Net(send, recv, own_sem)
     rows, width = hidden.shape
@@ -230,14 +231,24 @@
     wv.start()
     wk.start()
 
-    angle = (
-        places[:, 0:1] * rates[0:1] + places[:, 1:2] * rates[1:2] + places[:, 2:3] * rates[2:3]
-    )
+    def column(line):
+        return jnp.broadcast_to(line, (HEAD_DIM, line.shape[1])).T
+
+    angle = jnp.zeros((rows, HEAD_DIM), jnp.float32)
+    for i in range(3):
+        angle = angle + column(positions[i : i + 1, :].astype(jnp.float32)) * rates[i : i + 1]
     lane = lax.broadcasted_iota(jnp.int32, angle.shape, 1)
     even = lane % 2 == 0
     tables[0] = jnp.cos(angle)
     sine = jnp.sin(angle)
     tables[1] = jnp.where(even, -sine, sine)
+
+    @pl.loop(0, segs.shape[0])
+    def _(i):
+        numbers = column(segs[pl.ds(i, 1), :].astype(jnp.float32))
+        lanes = lax.broadcasted_iota(jnp.int32, numbers.shape, 1).astype(jnp.float32)
+        part = pl.ds(pl.multiple_of(i * HEAD_DIM, HEAD_DIM), HEAD_DIM)
+        marks[part, :] = jnp.where(numbers == lanes, 0.0, -1.0).astype(jnp.bfloat16)
 
     def normalise():
         net.locals[0].wait()
@@ -286,26 +297,82 @@
         for i, device in enumerate(net.peers()):
             net.put(mine, mine, ("sq", number, i), device)
 
-    def turned(number, gain):
+    def turned(number, gain, scale):
         others = [(p, s) for p in (0, 1) for s in range(4) if (p, s) != (0, 0)]
         for i, (pair, step) in enumerate(others):
             net.got(squares.at[number, net.col_at(pair, -step)], ("sq", number, i))
         total = jnp.sum(squares[number], axis=0)
-        column = jnp.broadcast_to(total[0:1], (HEAD_DIM, rows)).T
-        factor = lax.rsqrt(column / features + epsilon)
+        factor = lax.rsqrt(column(total[0:1]) / features + epsilon) * scale
         made = []
         for h in range(heads):
-            part = slice(h * HEAD_DIM, (h + 1) * HEAD_DIM)
-            normed = raw[:, part] * factor * gain[0:1, part]
+            normed = raw[:, h * HEAD_DIM : (h + 1) * HEAD_DIM] * factor * gain[h : h + 1, :]
             swapped = jnp.where(
                 even, pltpu.roll(normed, HEAD_DIM - 1, 1), pltpu.roll(normed, 1, 1)
             )
             made.append((normed * tables[0] + swapped * tables[1]).astype(jnp.bfloat16))
-        return jnp.concatenate(made, axis=1)
-
-    pull(wv.events(), wk.events(), hid.events())
+        return made
+
+    def loads(chip, slot):
+        for i, (source, target) in enumerate(((keys_all, key_buf), (values_all, value_buf))):
+            for core in range(2):
+                yield pltpu.make_async_copy(
+                    source.at[chip * 2 + core],
+                    target.at[slot, pl.ds(core * rows, rows)],
+                    load_sem.at[slot, 2 * i + core],
+                )
+
+    ones = jnp.ones((2 * rows, HEAD_DIM), jnp.bfloat16)
+
+    def attend(chip, slot):
+        for copy in loads(chip, slot):
+            copy.wait()
+        key_marks = marks[pl.ds(pl.multiple_of(chip * 2 * rows, HEAD_DIM), 2 * rows), :]
+        for h in range(heads):
+            part = slice(h * HEAD_DIM, (h + 1) * HEAD_DIM)
+            scores = lax.dot_general(
+                query_own[h],
+                jnp.concatenate([key_buf[slot, :, part], key_marks], axis=1),
+                (((1,), (1,)), ((), ())),
+                preferred_element_type=jnp.float32,
+            )
+            old = top[h]
+            new = jnp.maximum(old, jnp.max(scores, axis=1, keepdims=True))
+            top[h] = new
+            chances = jnp.exp2(scores - new[:, 0:1])
+            factor = jnp.exp2(old - new)
+            mixed = jnp.dot(
+                chances.astype(jnp.bfloat16),
+                jnp.concatenate([value_buf[slot, :, part], ones], axis=1),
+                preferred_element_type=jnp.float32,
+            )
+            acc[h] = acc[h] * jnp.concatenate([factor, factor], axis=1) + mixed
+
+    waiting = []
+
+    def block(pair, step):
+        chip = net.row_at(pair, step, False) // 2
+        if (pair, step) == (0, 0):
+            for copy in net.locals[4:6]:
+                copy.wait()
+        for ring in (kk, vv):
+            ring.met(pair, step)
+        slot = block_count[0] % 2
+        block_count[0] += 1
+        for copy in loads(chip, slot):
+            copy.start()
+        if waiting:
+            attend(*waiting.pop())
+        waiting.append((chip, slot))
+
+    block_count = [0]
+
+    v_steps, k_steps, q_steps = wv.events(), wk.events(), wq.events()
+    x_steps = hid.events()
+    pull(v_steps[:5], k_steps[:5], x_steps[:5])
     wq.start()
+    pull(v_steps[5:6], k_steps[5:6], x_steps[5:7])
     normalise()
+    pull(v_steps[6:7], k_steps[6:7])
     wv.finish()
     for copy in net.locals[1:3]:
         copy.wait()
@@ -315,38 +382,98 @@
     wk.finish()
     project(1)
     send_squares(0)
-    queue = wq.events()
-    for event in queue[:3]:
-        event()
-    key_own[...] = turned(0, k_gain)
+    pull(q_steps[:3])
+    key_own[...] = jnp.concatenate(turned(0, k_gain, 1.0), axis=1)
     kk.start()
-    pull(queue[3:], vv.events(), kk.events())
+    v_steps, k_steps = vv.events(), kk.events()
+    pull(q_steps[3:], v_steps[:3], k_steps[:3])
     wq.finish()
     net.locals[3].wait()
     project(0)
     send_squares(1)
-    query_out[...] = turned(1, q_gain)
-    vv.finish()
-    kk.finish()
-    for copy in net.locals[4:]:
-        copy.wait()
+    top[...] = jnp.full_like(top, -1e20)
+    acc[...] = jnp.zeros_like(acc)
+    pull(v_steps[3:4], k_steps[3:5])
+    own_start = pl.multiple_of(net.row * rows, HEAD_DIM)
+    own_marks = marks[pl.ds(own_start, rows), :].astype(jnp.float32)
+    query_marks = ((own_marks + 1.0) * 1e30).astype(jnp.bfloat16)
+    for h, piece in enumerate(turned(1, q_gain, HEAD_DIM ** (-0.5) * LOG2E)):
+        query_own[h] = jnp.concatenate([piece, query_marks], axis=1)
+    block(0, 0)
+    block(0, -1)
+    block(0, 1)
+    pull(v_steps[4:6], k_steps[5:6])
+    block(1, 0)
+    block(1, -1)
+    block(1, 1)
+    pull(v_steps[6:7], k_steps[6:7])
+    block(0, 2)
+    block(1, 2)
+    attend(*waiting.pop())
+    for h in range(heads):
+        part = slice(h * HEAD_DIM, (h + 1) * HEAD_DIM)
+        attended[:, part] = (acc[h, :, :HEAD_DIM] / acc[h, :, HEAD_DIM:]).astype(attended.dtype)
     for copy in net.sent:
         copy.wait_send()
 
 
-def project(hidden, modulation, w_query, w_key, w_value, q_gain, k_gain, positions):
+def pages_kernel(page_table, result, keys, values, attended, pages, sem):
+    own_pages = pages.shape[1]
+    first = lax.axis_index("row") * own_pages
+
+    def look(b, found):
+        return tuple(
+            jnp.where(page_table[b] == first + j, b, found[j]) for j in range(own_pages)
+        )
+
+    start = tuple(jnp.int32(0) for _ in range(own_pages))
+    found = lax.fori_loop(0, page_table.shape[0], look, start)
+    copies = [pltpu.make_async_copy(result, attended, sem.at[2 * own_pages])]
+    for i, source in enumerate((keys, values)):
+        for j in range(own_pages):
+            rows = pl.ds(pl.multiple_of(found[j] * PAGE, PAGE), PAGE)
+            copies.append(
+                pltpu.make_async_copy(source.at[rows], pages.at[i, j], sem.at[i * own_pages + j])
+            )
+    for copy in copies:
+        copy.start()
+    for copy in copies:
+        copy.wait()
+
+
+def store_pages(page_table, result, keys, values):
+    rows, width = result.shape
+    any_spec = pl.BlockSpec(memory_space=pl.ANY)
+    own_pages = rows // PAGE
+    return pl.pallas_call(
+        pages_kernel,
+        out_shape=(
+            jax.ShapeDtypeStruct((rows, width), jnp.bfloat16),
+            jax.ShapeDtypeStruct((2, own_pages, PAGE, width), jnp.bfloat16),
+        ),
+        in_specs=[pl.BlockSpec(memory_space=pltpu.SMEM), any_spec, any_spec, any_spec],
+        out_specs=(any_spec, any_spec),
+        scratch_shapes=[pltpu.SemaphoreType.DMA((2 * own_pages + 1,))],
+        compiler_params=pltpu.CompilerParams(vmem_limit_bytes=60 * 2**20),
+        name="pages",
+    )(page_table, result, keys, values)
+
+
+def body(
+    hidden, modulation, w_query, w_key, w_value, q_gain, k_gain, positions, segment_ids, page_table
+):
     rows, width = hidden.shape
     deep = w_query.shape[0]
     features = modulation.shape[1]
-    members, groups = features // deep, features // width
-    places = positions.astype(jnp.float32).T
+    tokens = segment_ids.shape[0]
+    members, groups, heads = features // deep, features // width, width // HEAD_DIM
     any_spec = pl.BlockSpec(memory_space=pl.ANY)
     vmem = pl.BlockSpec(memory_space=pltpu.VMEM)
-    tokens = jax.ShapeDtypeStruct((members, rows, width), jnp.bfloat16)
-    return pl.pallas_call(
-        project_kernel,
-        out_shape=(jax.ShapeDtypeStruct((rows, width), jnp.bfloat16), tokens, tokens),
-        in_specs=[vmem, vmem, any_spec, any_spec, any_spec, vmem, vmem, vmem, vmem],
+    shards = jax.ShapeDtypeStruct((members, rows, width), jnp.bfloat16)
+    attended, keys, values = pl.pallas_call(
+        attention_kernel,
+        out_shape=(jax.ShapeDtypeStruct((rows, width), jnp.bfloat16), shards, shards),
+        in_specs=[any_spec, vmem, any_spec, any_spec, any_spec, vmem, vmem, vmem, vmem, vmem],
         out_specs=(vmem, any_spec, any_spec),
         scratch_shapes=[
             pltpu.VMEM((groups, rows, width), jnp.bfloat16),
@@ -357,148 +484,29 @@
             pltpu.VMEM((rows, width), jnp.bfloat16),
             pltpu.VMEM((2, groups, 8, rows), jnp.float32),
             pltpu.VMEM((2, rows, HEAD_DIM), jnp.float32),
+            pltpu.VMEM((heads, rows, 2 * HEAD_DIM), jnp.bfloat16),
+            pltpu.VMEM((tokens, HEAD_DIM), jnp.bfloat16),
+            pltpu.VMEM((2, 2 * rows, width), jnp.bfloat16),
+            pltpu.VMEM((2, 2 * rows, width), jnp.bfloat16),
+            pltpu.VMEM((heads, rows, HEAD_DIM), jnp.float32),
+            pltpu.VMEM((heads, rows, 2 * HEAD_DIM), jnp.float32),
             pltpu.SemaphoreType.DMA((128,)),
             pltpu.SemaphoreType.DMA((128,)),
             pltpu.SemaphoreType.DMA((6,)),
+            pltpu.SemaphoreType.DMA((2, 4)),
         ],
         compiler_params=pltpu.CompilerParams(
-            collective_id=0, has_side_effects=True, vmem_limit_bytes=56 * 2**20
+            collective_id=0, has_side_effects=True, vmem_limit_bytes=58 * 2**20
         ),
-        name="project",
+        name="attention",
     )(
-        hidden, modulation, w_query, w_key, w_value, q_gain[None], k_gain[None], places,
+        hidden, modulation, w_query, w_key, w_value,
+        q_gain.reshape(heads, HEAD_DIM), k_gain.reshape(heads, HEAD_DIM), positions,
+        segment_ids.reshape(tokens // HEAD_DIM, HEAD_DIM),
         jnp.asarray(rotary_rates(HEAD_DIM // 2)),
     )
-
-
-def attend_kernel(
-    plan, query, keys, values, query_segs, key_segs, attended, pages,
-    key_buf, value_buf, top, acc, load_sem, page_sem,
-):
-    rows, width = query.shape
-    heads = width // HEAD_DIM
-    block = KEY_BLOCK
-    own_pages = pages.shape[1]
-    lo, hi = plan[0], plan[1]
-
-    def page_copy(which, j):
-        source = (keys, values)[which]
-        start = pl.multiple_of(plan[2 + j] * PAGE, PAGE)
-        return pltpu.make_async_copy(
-            source.at[pl.ds(start, PAGE)], pages.at[which, j], page_sem.at[which, j]
-        )
-
-    def load(number, slot):
-        start = pl.multiple_of(number * block, block)
-        return (
-            pltpu.make_async_copy(
-                keys.at[pl.ds(start, block)], key_buf.at[slot], load_sem.at[0, slot]
-            ),
-            pltpu.make_async_copy(
-                values.at[pl.ds(start, block)], value_buf.at[slot], load_sem.at[1, slot]
-            ),
-        )
-
-    for copy in load(lo, 0):
-        copy.start()
-    for which in range(2):
-        for j in range(own_pages):
-            page_copy(which, j).start()
-    top[...] = jnp.full_like(top, -1e30)
-    acc[...] = jnp.zeros_like(acc)
-    ones = jnp.ones((block, HEAD_DIM), jnp.bfloat16)
-    scale = HEAD_DIM ** (-0.5) * LOG2E
-
-    @pl.loop(lo, hi)
-    def _(number):
-        slot = lax.rem(number - lo, 2)
-        for copy in load(number, slot):
-            copy.wait()
-
-        @pl.when(number + 1 < hi)
-        def _():
-            for copy in load(number + 1, 1 - slot):
-                copy.start()
-
-        allowed = query_segs[:, 0:1] == key_segs[number]
-        for h in range(heads):
-            part = pl.ds(h * HEAD_DIM, HEAD_DIM)
-            scores = lax.dot_general(
-                query[:, part], key_buf[slot, :, part], (((1,), (1,)), ((), ())),
-                preferred_element_type=jnp.float32,
-            ) * scale
-            scores = jnp.where(allowed, scores, -1e30)
-            old = top[h]
-            new = jnp.maximum(old, jnp.max(scores, axis=1, keepdims=True))
-            top[h] = new
-            weights = jnp.where(allowed, jnp.exp2(scores - new[:, 0:1]), 0.0)
-            factor = jnp.exp2(old - new)
-            mixed = jnp.dot(
-                weights.astype(jnp.bfloat16),
-                jnp.concatenate([value_buf[slot, :, part], ones], axis=1),
-                preferred_element_type=jnp.float32,
-            )
-            acc[h] = acc[h] * jnp.concatenate([factor, factor], axis=1) + mixed
-
-    for h in range(heads):
-        part = pl.ds(h * HEAD_DIM, HEAD_DIM)
-        attended[:, part] = (acc[h, :, :HEAD_DIM] / acc[h, :, HEAD_DIM:]).astype(attended.dtype)
-    for which in range(2):
-        for j in range(own_pages):
-            page_copy(which, j).wait()
-
-
-def attend(query, keys, values, segment_ids, page_table):
-    rows, width = query.shape
-    heads = width // HEAD_DIM
-    tokens = keys.shape[0]
-    row = lax.axis_index("row")
-    query_segs = lax.dynamic_slice_in_dim(segment_ids, row * rows, rows, 0)
-    first, last = query_segs[0], query_segs[-1]
-    lo = jnp.sum(segment_ids < first) // KEY_BLOCK
-    hi = (jnp.sum(segment_ids <= last) + KEY_BLOCK - 1) // KEY_BLOCK
-    own_pages = rows // PAGE
-    slots = row * own_pages + jnp.arange(own_pages)
-    numbers = jnp.arange(page_table.shape[0], dtype=jnp.int32)
-    owned = jnp.sum(jnp.where(page_table[None] == slots[:, None], numbers[None], 0), axis=1)
-    plan = jnp.concatenate([jnp.stack([lo, hi]).astype(jnp.int32), owned.astype(jnp.int32)])
-    any_spec = pl.BlockSpec(memory_space=pl.ANY)
-    vmem = pl.BlockSpec(memory_space=pltpu.VMEM)
-    return pl.pallas_call(
-        attend_kernel,
-        out_shape=(
-            jax.ShapeDtypeStruct((rows, width), jnp.bfloat16),
-            jax.ShapeDtypeStruct((2, own_pages, PAGE, width), jnp.bfloat16),
-        ),
-        in_specs=[
-            pl.BlockSpec(memory_space=pltpu.SMEM), vmem, any_spec, any_spec, vmem, vmem,
-        ],
-        out_specs=(vmem, any_spec),
-        scratch_shapes=[
-            pltpu.VMEM((2, KEY_BLOCK, width), jnp.bfloat16),
-            pltpu.VMEM((2, KEY_BLOCK, width), jnp.bfloat16),
-            pltpu.VMEM((heads, rows, HEAD_DIM), jnp.float32),
-            pltpu.VMEM((heads, rows, 2 * HEAD_DIM), jnp.float32),
-            pltpu.SemaphoreType.DMA((2, 2)),
-            pltpu.SemaphoreType.DMA((2, own_pages)),
-        ],
-        compiler_params=pltpu.CompilerParams(vmem_limit_bytes=40 * 2**20),
-        name="attend",
-    )(
-        plan, query, keys, values, query_segs[:, None],
-        segment_ids.reshape(tokens // KEY_BLOCK, 1, KEY_BLOCK),
-    )
-
-
-def body(
-    hidden, modulation, w_query, w_key, w_value, q_gain, k_gain, positions, segment_ids, page_table
-):
-    query, keys, values = project(
-        hidden, modulation, w_query, w_key, w_value, q_gain, k_gain, positions
-    )
-    tokens, width = segment_ids.shape[0], hidden.shape[1]
-    return attend(
-        query, keys.reshape(tokens, width), values.reshape(tokens, width), segment_ids, page_table
+    return store_pages(
+        page_table, attended, keys.reshape(tokens, width), values.reshape(tokens, width)
     )
 
 

time: 191 us -> 209 us (1.094)
  Pallas kernels: 171 us -> 208 us
  local copies, waits for them, and re-layouts: 9.82 us -> 0 us
  other arithmetic: 4.36 us -> 0 us
  between operations: 4.03 us -> 0.82 us
    pallas_call x2, Pallas kernels: 171 us -> 208 us  [the longest x1 161 us: body(): pl.pallas_call(attention_kernel, out_shape=(jax.ShapeDtypeStruct((rows, w...]
    unnamed x6 -> x0, local copies, waits for them, and re-layouts: 4.99 us -> none
    reduce_sum x2 -> x0, other arithmetic: 3.59 us -> none  [the longest x1 2.75 us: attend(): lo = jnp.sum(segment_ids < first) // KEY_BLOCK]
    broadcast_in_dim x3 -> x0, local copies, waits for them, and re-layouts: 2.65 us -> none  [the longest x1 1.28 us: project(): k_gain[None]]
where the time goes in v3:
time: 209 us; the launch traced here: 208 us
  Pallas kernels  208 us (100%)
    pallas_call x1, Pallas kernels, body(): pl.pallas_call(attention_kernel, out_shape=(jax.ShapeDtypeStruct((rows, w...  161 us
    pallas_call x1, Pallas kernels, store_pages(): pl.pallas_call(pages_kernel, out_shape=(jax.ShapeDtypeStruct((rows, width...  47.1 us

profile of v3, /device:TPU:1, one launch (start us, length us, event | category | flops | bytes accessed | tf_op | source)
XLA Modules:
  0.0 208.4 jit_solution(12443798488445813983)
XLA Ops:
  0.6 160.5 %attention.1 = (bf16[384,640]{1,0:T(8,128)(2,1)}, bf16[16,384,640]{2,1,0:T(8,128)(2,1)}, bf16[16,384,640]{2,1,0:T(8,128)(2,1)}) custom-call(bf16[384,640]{1,0:T(8,128)(2,1)} %hidden.1, f32[2,5120]{1,0:T(2,128)} %modulation.1, bf16[320,640]{1,0:T(8,128)(2,1)} %w_query.1, bf16[320,640]{1,0:T(8,128)(2,1)} %w_key.1, bf16[320,640]{1,0:T(8,128)(2,1)} %w_value.1, ...), custom_call_target="tpu_custom_call" | custom-call | tf_op jit(solution)/shard_map/attention/pallas_call | solution.py:473
  161.2 47.1 %pages.1 = (bf16[384,640]{1,0:T(8,128)(2,1)}, bf16[2,3,128,640]{3,2,1,0:T(8,128)(2,1)}) custom-call(s32[48]{0:T(128)} %page_table.1, bf16[384,640]{1,0:T(8,128)(2,1)} %get-tuple-element.5.result, bf16[6144,640]{1,0:T(8,128)(2,1)} %bitcast.5, bf16[6144,640]{1,0:T(8,128)(2,1)} %bitcast.6), custom_call_target="tpu_custom_call" | custom-call | tf_op jit(solution)/shard_map/pages/pallas_call | solution.py:448

commit v4 on v3

--- a/solution.py
+++ b/solution.py
@@ -211,7 +211,7 @@
         return lambda slot, half: weights.at[which, cut(slot * deep, deep, half)]
 
     def token_view(ref):
-        return lambda slot, half: ref.at[slot, cut(0, rows, half)]
+        return lambda slot, half: ref.at[slot, cut(0, ref.shape[1], half)]
 
     hid = Ring(net, "x", hidden, token_view(hidden_all), True, False)
     wk = Ring(net, "wk", w_key, weight_view(1), True, True)
@@ -245,10 +245,10 @@
 
     @pl.loop(0, segs.shape[0])
     def _(i):
-        numbers = column(segs[pl.ds(i, 1), :].astype(jnp.float32))
-        lanes = lax.broadcasted_iota(jnp.int32, numbers.shape, 1).astype(jnp.float32)
+        numbers = jnp.broadcast_to(segs[pl.ds(i, 1), :], (HEAD_DIM, HEAD_DIM))
+        kinds = lax.broadcasted_iota(jnp.int32, numbers.shape, 0)
         part = pl.ds(pl.multiple_of(i * HEAD_DIM, HEAD_DIM), HEAD_DIM)
-        marks[part, :] = jnp.where(numbers == lanes, 0.0, -1.0).astype(jnp.bfloat16)
+        marks[:, part] = jnp.where(numbers == kinds, 0.0, -1.0).astype(jnp.bfloat16)
 
     def normalise():
         net.locals[0].wait()
@@ -309,7 +309,7 @@
             swapped = jnp.where(
                 even, pltpu.roll(normed, HEAD_DIM - 1, 1), pltpu.roll(normed, 1, 1)
             )
-            made.append((normed * tables[0] + swapped * tables[1]).astype(jnp.bfloat16))
+            made.append(normed * tables[0] + swapped * tables[1])
         return made
 
     def loads(chip, slot):
@@ -317,7 +317,7 @@
             for core in range(2):
                 yield pltpu.make_async_copy(
                     source.at[chip * 2 + core],
-                    target.at[slot, pl.ds(core * rows, rows)],
+                    target.at[slot, core],
                     load_sem.at[slot, 2 * i + core],
                 )
 
@@ -326,13 +326,14 @@
     def attend(chip, slot):
         for copy in loads(chip, slot):
             copy.wait()
-        key_marks = marks[pl.ds(pl.multiple_of(chip * 2 * rows, HEAD_DIM), 2 * rows), :]
+        chip_start = pl.multiple_of(chip * 2 * rows, HEAD_DIM)
+        key_marks = marks[:, pl.ds(chip_start, 2 * rows)]
         for h in range(heads):
             part = slice(h * HEAD_DIM, (h + 1) * HEAD_DIM)
-            scores = lax.dot_general(
+            keys = jnp.concatenate([key_buf[slot, 0, part], key_buf[slot, 1, part]], axis=1)
+            scores = jnp.dot(
                 query_own[h],
-                jnp.concatenate([key_buf[slot, :, part], key_marks], axis=1),
-                (((1,), (1,)), ((), ())),
+                jnp.concatenate([keys, key_marks], axis=0),
                 preferred_element_type=jnp.float32,
             )
             old = top[h]
@@ -342,7 +343,9 @@
             factor = jnp.exp2(old - new)
             mixed = jnp.dot(
                 chances.astype(jnp.bfloat16),
-                jnp.concatenate([value_buf[slot, :, part], ones], axis=1),
+                jnp.concatenate(
+                    [value_buf[slot, :, :, part].reshape(2 * rows, HEAD_DIM), ones], axis=1
+                ),
                 preferred_element_type=jnp.float32,
             )
             acc[h] = acc[h] * jnp.concatenate([factor, factor], axis=1) + mixed
@@ -383,7 +386,8 @@
     project(1)
     send_squares(0)
     pull(q_steps[:3])
-    key_own[...] = jnp.concatenate(turned(0, k_gain, 1.0), axis=1)
+    for h, piece in enumerate(turned(0, k_gain, 1.0)):
+        key_own[h * HEAD_DIM : (h + 1) * HEAD_DIM, :] = piece.T.astype(jnp.bfloat16)
     kk.start()
     v_steps, k_steps = vv.events(), kk.events()
     pull(q_steps[3:], v_steps[:3], k_steps[:3])
@@ -394,11 +398,17 @@
     top[...] = jnp.full_like(top, -1e20)
     acc[...] = jnp.zeros_like(acc)
     pull(v_steps[3:4], k_steps[3:5])
-    own_start = pl.multiple_of(net.row * rows, HEAD_DIM)
-    own_marks = marks[pl.ds(own_start, rows), :].astype(jnp.float32)
-    query_marks = ((own_marks + 1.0) * 1e30).astype(jnp.bfloat16)
+    own_lines = rows // HEAD_DIM
+    numbers = jnp.concatenate(
+        [
+            column(segs[pl.ds(net.row * own_lines + i, 1), :].astype(jnp.float32))
+            for i in range(own_lines)
+        ],
+        axis=0,
+    )
+    query_marks = jnp.where(numbers == lane.astype(jnp.float32), 1e30, 0.0).astype(jnp.bfloat16)
     for h, piece in enumerate(turned(1, q_gain, HEAD_DIM ** (-0.5) * LOG2E)):
-        query_own[h] = jnp.concatenate([piece, query_marks], axis=1)
+        query_own[h] = jnp.concatenate([piece.astype(jnp.bfloat16), query_marks], axis=1)
     block(0, 0)
     block(0, -1)
     block(0, 1)
@@ -406,8 +416,9 @@
     block(1, 0)
     block(1, -1)
     block(1, 1)
+    block(0, 2)
+    attend(*waiting.pop())
     pull(v_steps[6:7], k_steps[6:7])
-    block(0, 2)
     block(1, 2)
     attend(*waiting.pop())
     for h in range(heads):
@@ -417,8 +428,9 @@
         copy.wait_send()
 
 
-def pages_kernel(page_table, result, keys, values, attended, pages, sem):
+def pages_kernel(page_table, result, keys, values, attended, pages, turned, sem):
     own_pages = pages.shape[1]
+    blocks = keys.shape[2] // PAGE
     first = lax.axis_index("row") * own_pages
 
     def look(b, found):
@@ -428,22 +440,31 @@
 
     start = tuple(jnp.int32(0) for _ in range(own_pages))
     found = lax.fori_loop(0, page_table.shape[0], look, start)
-    copies = [pltpu.make_async_copy(result, attended, sem.at[2 * own_pages])]
-    for i, source in enumerate((keys, values)):
-        for j in range(own_pages):
-            rows = pl.ds(pl.multiple_of(found[j] * PAGE, PAGE), PAGE)
-            copies.append(
-                pltpu.make_async_copy(source.at[rows], pages.at[i, j], sem.at[i * own_pages + j])
+    copies = []
+    for j in range(own_pages):
+        shard = found[j] // blocks
+        part = pl.ds(pl.multiple_of((found[j] - shard * blocks) * PAGE, PAGE), PAGE)
+        copies.append(
+            pltpu.make_async_copy(keys.at[shard, :, part], turned.at[j], sem.at[j])
+        )
+        copies.append(
+            pltpu.make_async_copy(
+                values.at[shard, part], pages.at[1, j], sem.at[own_pages + j]
             )
+        )
     for copy in copies:
         copy.start()
+    attended[...] = result[...]
     for copy in copies:
         copy.wait()
+    for j in range(own_pages):
+        pages[0, j] = turned[j].T
 
 
 def store_pages(page_table, result, keys, values):
     rows, width = result.shape
     any_spec = pl.BlockSpec(memory_space=pl.ANY)
+    vmem = pl.BlockSpec(memory_space=pltpu.VMEM)
     own_pages = rows // PAGE
     return pl.pallas_call(
         pages_kernel,
@@ -451,9 +472,12 @@
             jax.ShapeDtypeStruct((rows, width), jnp.bfloat16),
             jax.ShapeDtypeStruct((2, own_pages, PAGE, width), jnp.bfloat16),
         ),
-        in_specs=[pl.BlockSpec(memory_space=pltpu.SMEM), any_spec, any_spec, any_spec],
-        out_specs=(any_spec, any_spec),
-        scratch_shapes=[pltpu.SemaphoreType.DMA((2 * own_pages + 1,))],
+        in_specs=[pl.BlockSpec(memory_space=pltpu.SMEM), vmem, any_spec, any_spec],
+        out_specs=(vmem, vmem),
+        scratch_shapes=[
+            pltpu.VMEM((own_pages, width, PAGE), jnp.bfloat16),
+            pltpu.SemaphoreType.DMA((2 * own_pages,)),
+        ],
         compiler_params=pltpu.CompilerParams(vmem_limit_bytes=60 * 2**20),
         name="pages",
     )(page_table, result, keys, values)
@@ -469,10 +493,13 @@
     members, groups, heads = features // deep, features // width, width // HEAD_DIM
     any_spec = pl.BlockSpec(memory_space=pl.ANY)
     vmem = pl.BlockSpec(memory_space=pltpu.VMEM)
-    shards = jax.ShapeDtypeStruct((members, rows, width), jnp.bfloat16)
+    key_shards = jax.ShapeDtypeStruct((members, width, rows), jnp.bfloat16)
+    value_shards = jax.ShapeDtypeStruct((members, rows, width), jnp.bfloat16)
     attended, keys, values = pl.pallas_call(
         attention_kernel,
-        out_shape=(jax.ShapeDtypeStruct((rows, width), jnp.bfloat16), shards, shards),
+        out_shape=(
+            jax.ShapeDtypeStruct((rows, width), jnp.bfloat16), key_shards, value_shards
+        ),
         in_specs=[any_spec, vmem, any_spec, any_spec, any_spec, vmem, vmem, vmem, vmem, vmem],
         out_specs=(vmem, any_spec, any_spec),
         scratch_shapes=[
@@ -480,14 +507,14 @@
             pltpu.VMEM((rows, features), jnp.bfloat16),
             pltpu.VMEM((3, features, width), jnp.bfloat16),
             pltpu.VMEM((rows, width), jnp.float32),
-            pltpu.VMEM((rows, width), jnp.bfloat16),
+            pltpu.VMEM((width, rows), jnp.bfloat16),
             pltpu.VMEM((rows, width), jnp.bfloat16),
             pltpu.VMEM((2, groups, 8, rows), jnp.float32),
             pltpu.VMEM((2, rows, HEAD_DIM), jnp.float32),
             pltpu.VMEM((heads, rows, 2 * HEAD_DIM), jnp.bfloat16),
-            pltpu.VMEM((tokens, HEAD_DIM), jnp.bfloat16),
-            pltpu.VMEM((2, 2 * rows, width), jnp.bfloat16),
-            pltpu.VMEM((2, 2 * rows, width), jnp.bfloat16),
+            pltpu.VMEM((HEAD_DIM, tokens), jnp.bfloat16),
+            pltpu.VMEM((2, 2, width, rows), jnp.bfloat16),
+            pltpu.VMEM((2, 2, rows, width), jnp.bfloat16),
             pltpu.VMEM((heads, rows, HEAD_DIM), jnp.float32),
             pltpu.VMEM((heads, rows, 2 * HEAD_DIM), jnp.float32),
             pltpu.SemaphoreType.DMA((128,)),
@@ -505,9 +532,7 @@
         segment_ids.reshape(tokens // HEAD_DIM, HEAD_DIM),
         jnp.asarray(rotary_rates(HEAD_DIM // 2)),
     )
-    return store_pages(
-        page_table, attended, keys.reshape(tokens, width), values.reshape(tokens, width)
-    )
+    return store_pages(page_table, attended, keys, values)
 
 
 def solution(mesh):

time: 209 us -> 169 us (0.81)
  Pallas kernels: 208 us -> 168 us
    pallas_call x1, Pallas kernels: 47.1 us -> 4.1 us  [store_pages(): pl.pallas_call(pages_kernel, out_shape=(jax.ShapeDtypeStruct((rows, width...]
    pallas_call x1, Pallas kernels: 161 us -> 164 us  [body(): pl.pallas_call(attention_kernel, out_shape=(jax.ShapeDtypeStruct((rows, w...]
where the time goes in v4:
time: 169 us
  Pallas kernels  168 us (99%)
    pallas_call x1, Pallas kernels, body(): pl.pallas_call(attention_kernel, out_shape=(jax.ShapeDtypeStruct((rows, w...  164 us
    pallas_call x1, Pallas kernels, store_pages(): pl.pallas_call(pages_kernel, out_shape=(jax.ShapeDtypeStruct((rows, width...  4.1 us

profile of v4, /device:TPU:1, one launch (start us, length us, event | category | flops | bytes accessed | tf_op | source)
XLA Modules:
  0.0 168.9 jit_solution(10067285917736369673)
XLA Ops:
  0.6 164.0 %attention.1 = (bf16[384,640]{1,0:T(8,128)(2,1)}, bf16[16,640,384]{2,1,0:T(8,128)(2,1)}, bf16[16,384,640]{2,1,0:T(8,128)(2,1)}) custom-call(bf16[384,640]{1,0:T(8,128)(2,1)} %hidden.1, f32[2,5120]{1,0:T(2,128)} %modulation.1, bf16[320,640]{1,0:T(8,128)(2,1)} %w_query.1, bf16[320,640]{1,0:T(8,128)(2,1)} %w_key.1, bf16[320,640]{1,0:T(8,128)(2,1)} %w_value.1, ...), custom_call_target="tpu_custom_call" | custom-call | tf_op jit(solution)/shard_map/attention/pallas_call | solution.py:498
  164.6 4.1 %pages.1 = (bf16[384,640]{1,0:T(8,128)(2,1)}, bf16[2,3,128,640]{3,2,1,0:T(8,128)(2,1)}) custom-call(s32[48]{0:T(128)} %page_table.1, bf16[384,640]{1,0:T(8,128)(2,1)} %get-tuple-element.5.result, bf16[16,640,384]{2,1,0:T(8,128)(2,1)} %get-tuple-element.6.keys, bf16[16,384,640]{2,1,0:T(8,128)(2,1)} %get-tuple-element.7.values), custom_call_target="tpu_custom_call" | custom-call | tf_op jit(solution)/shard_map/pages/pallas_call | solution.py:469

commit v5 on v4

--- a/solution.py
+++ b/solution.py
@@ -452,13 +452,15 @@
                 values.at[shard, part], pages.at[1, j], sem.at[own_pages + j]
             )
         )
+    copies.append(pltpu.make_async_copy(result, attended, sem.at[2 * own_pages]))
     for copy in copies:
         copy.start()
-    attended[...] = result[...]
-    for copy in copies:
-        copy.wait()
     for j in range(own_pages):
+        copies[2 * j].wait()
         pages[0, j] = turned[j].T
+    for j in range(own_pages):
+        copies[2 * j + 1].wait()
+    copies[-1].wait()
 
 
 def store_pages(page_table, result, keys, values):
@@ -472,11 +474,11 @@
             jax.ShapeDtypeStruct((rows, width), jnp.bfloat16),
             jax.ShapeDtypeStruct((2, own_pages, PAGE, width), jnp.bfloat16),
         ),
-        in_specs=[pl.BlockSpec(memory_space=pltpu.SMEM), vmem, any_spec, any_spec],
+        in_specs=[pl.BlockSpec(memory_space=pltpu.SMEM), any_spec, any_spec, any_spec],
         out_specs=(vmem, vmem),
         scratch_shapes=[
             pltpu.VMEM((own_pages, width, PAGE), jnp.bfloat16),
-            pltpu.SemaphoreType.DMA((2 * own_pages,)),
+            pltpu.SemaphoreType.DMA((2 * own_pages + 1,)),
         ],
         compiler_params=pltpu.CompilerParams(vmem_limit_bytes=60 * 2**20),
         name="pages",

time: 169 us -> 169 us (level)
  no operation moved by 1% of the time
where the time goes in v5:
time: 169 us
  Pallas kernels  168 us (99%)
    pallas_call x1, Pallas kernels, body(): pl.pallas_call(attention_kernel, out_shape=(jax.ShapeDtypeStruct((rows, w...  164 us
    pallas_call x1, Pallas kernels, store_pages(): pl.pallas_call(pages_kernel, out_shape=(jax.ShapeDtypeStruct((rows, width...  3.86 us

profile of v5, /device:TPU:1, one launch (start us, length us, event | category | flops | bytes accessed | tf_op | source)
XLA Modules:
  0.0 168.7 jit_solution(17976016548726298625)
XLA Ops:
  0.6 164.0 %attention.1 = (bf16[384,640]{1,0:T(8,128)(2,1)}, bf16[16,640,384]{2,1,0:T(8,128)(2,1)}, bf16[16,384,640]{2,1,0:T(8,128)(2,1)}) custom-call(bf16[384,640]{1,0:T(8,128)(2,1)} %hidden.1, f32[2,5120]{1,0:T(2,128)} %modulation.1, bf16[320,640]{1,0:T(8,128)(2,1)} %w_query.1, bf16[320,640]{1,0:T(8,128)(2,1)} %w_key.1, bf16[320,640]{1,0:T(8,128)(2,1)} %w_value.1, ...), custom_call_target="tpu_custom_call" | custom-call | tf_op jit(solution)/shard_map/attention/pallas_call | solution.py:500
  164.6 3.9 %pages.1 = (bf16[384,640]{1,0:T(8,128)(2,1)}, bf16[2,3,128,640]{3,2,1,0:T(8,128)(2,1)}) custom-call(s32[48]{0:T(128)} %page_table.1, bf16[384,640]{1,0:T(8,128)(2,1)} %get-tuple-element.5.result, bf16[16,640,384]{2,1,0:T(8,128)(2,1)} %get-tuple-element.6.keys, bf16[16,384,640]{2,1,0:T(8,128)(2,1)} %get-tuple-element.7.values), custom_call_target="tpu_custom_call" | custom-call | tf_op jit(solution)/shard_map/pages/pallas_call | solution.py:471
